TPU v7x, 32 devices: a whole 2x2x4 slice. The times are simulated.
32 devices in a mesh: parts: 2 (over y), freq: 8 (over z, x), seg: 2 (over core).
Axes of the slice: x: 2, y: 2, z: 4, core: 2. Of those that a mesh axis runs over, the one named last changes fastest.
Arguments:
- samples: float32 [8, 2, 1024, 1024], P(('parts', 'seg'), None, 'freq'), parts along dimension 0, may hold values from -6 to 6
- kernels: bfloat16 [2, 8, 128], replicated, may hold values from -0.375 to 0.375
- offsets: int32 [8, 8], P(('parts', 'seg')), parts along dimension 0, may hold values from -4096 to 4096, as said below
- weight_index: int32 [8], P(('parts', 'seg')), parts along dimension 0, may hold values from 0 to 15
- level_weights: float32 [16], replicated, may hold values from 0.1 to 1
Outputs:
- planes: float32 [16, 1048576], P(('parts', 'seg'), 'freq'), parts along dimension 0
There are 2 independent parts, one for each index of `parts`. A program takes and returns all parts, laid end to end along the dimension named above; an argument that names none is the same for every part. Nothing has to cross between parts.
Inputs may be any that keep to these rules, and one draw needn't show every extreme that they name: `offsets`: each offset lies within 4096 blocks of zero; both ends are taken in every draw. Among the 16 offsets of one index of seg, at most 4 have the same quotient by 1024 (rounded down), and in every draw some quotient has exactly 4.
All inputs are finite; a program needn't handle non-finite values.
Results may differ from a plain program's by a relative error of at most 0.01.
Values may be sent and summed in bfloat16 or wider, within the bound.
A program may use at most 128 MiB of HBM per device.

v0:
```python
import math

import jax
import jax.numpy as jnp
from jax import lax
from jax.sharding import PartitionSpec as P

BLOCK = 128
KERNELS = 8
REACH = 4
ROUTE_CAP = 4


def extended(cells, sides, width):
    for axis, dim in sides:
        count = lax.axis_size(axis)
        head = lax.slice_in_dim(cells, 0, width, axis=dim)
        tail = lax.slice_in_dim(cells, cells.shape[dim] - width, cells.shape[dim], axis=dim)
        cells = jnp.concatenate(
            [
                lax.ppermute(tail, axis, [(i, (i + 1) % count) for i in range(count)]),
                cells,
                lax.ppermute(head, axis, [((i + 1) % count, i) for i in range(count)]),
            ],
            axis=dim,
        )
    return cells


def passed_along(block, axis, distance):
    devices = range(lax.axis_size(axis))
    route = [((i - distance) % len(devices), i) for i in devices]
    return lax.ppermute(block, axis, route)


def dft_table(size):
    rows = lax.broadcasted_iota(jnp.int32, (size, size), 0)
    cols = lax.broadcasted_iota(jnp.int32, (size, size), 1)
    angle = (rows * cols % size).astype(jnp.float32) * (2.0 * math.pi / size)
    return (jnp.cos(angle), jnp.sin(angle))


def toeplitz(kernels):
    width = kernels.shape[-1]
    tail = jnp.zeros(kernels.shape[:-1] + (width + 1,), kernels.dtype)
    padded = jnp.concatenate([kernels, tail], -1)
    tiled = jnp.tile(padded, (1, 1, width))[..., : 2 * width * width]
    return tiled.reshape(kernels.shape[:-1] + (width, 2 * width))


def take_blocks(joined, start):
    return lax.dynamic_slice_in_dim(joined, start, joined.shape[0] // 2, 0)


def slide(joined, starts):
    return jax.vmap(jax.vmap(take_blocks))(joined, starts)


def body(samples, kernels, offsets, weight_index, level_weights):
    segs, comps, rows_one, cols_two = samples.shape
    ranks = lax.axis_size("freq")
    here = lax.axis_index("freq")
    size_one = rows_one * ranks
    length = size_one * cols_two
    highest = lax.Precision.HIGHEST
    cos_two, sin_two = dft_table(cols_two)
    stacked = samples.reshape(segs * comps * rows_one, cols_two)
    with_cos = jnp.dot(stacked, cos_two, precision=highest).reshape(samples.shape)
    with_sin = jnp.dot(stacked, sin_two, precision=highest).reshape(samples.shape)
    first_real = with_cos[:, 0] + with_sin[:, 1]
    first_imag = with_cos[:, 1] - with_sin[:, 0]
    row_global = here * rows_one + lax.broadcasted_iota(jnp.int32, (rows_one, cols_two), 0)
    col_global = lax.broadcasted_iota(jnp.int32, (rows_one, cols_two), 1)
    twist = (row_global * col_global % length).astype(jnp.float32) * (2.0 * math.pi / length)
    twist_cos = jnp.cos(twist)
    twist_sin = jnp.sin(twist)
    turned = jnp.stack(
        [
            first_real * twist_cos + first_imag * twist_sin,
            first_imag * twist_cos - first_real * twist_sin,
        ],
        1,
    )
    columns = lax.all_to_all(
        turned.astype(jnp.bfloat16), "freq", split_axis=3, concat_axis=3, tiled=True
    ).astype(turned.dtype)
    width_two = cols_two // ranks
    ordered = columns.reshape(segs, comps, rows_one, ranks, width_two)
    cos_one, sin_one = dft_table(size_one)
    cos_one = cos_one.reshape(ranks, rows_one, size_one)
    sin_one = sin_one.reshape(ranks, rows_one, size_one)
    second_cos = jnp.einsum("scirl,rik->sclk", ordered, cos_one, precision=highest)
    second_sin = jnp.einsum("scirl,rik->sclk", ordered, sin_one, precision=highest)
    second = jnp.stack(
        [second_cos[:, 0] + second_sin[:, 1], second_cos[:, 1] - second_sin[:, 0]], 1
    )
    arrived = lax.all_to_all(
        second.astype(jnp.bfloat16), "freq", split_axis=3, concat_axis=3, tiled=True
    ).astype(second.dtype)
    width_one = size_one // ranks
    spectrum = arrived.reshape(segs, comps, width_two, ranks, width_one)
    spectrum = jnp.transpose(spectrum, (0, 1, 4, 3, 2)).reshape(segs, comps, width_one * cols_two)
    spectrum = (spectrum * (1.0 / math.sqrt(length))).astype(jnp.bfloat16)
    half = BLOCK // 2
    edged = extended(spectrum, (("freq", 2),), half)
    bins_here = spectrum.shape[2]
    count = bins_here // BLOCK
    lower = edged[..., :bins_here].reshape(segs, comps, count, BLOCK)
    upper = edged[..., BLOCK:].reshape(segs, comps, count, BLOCK)
    window = jnp.concatenate([lower, upper], -1)
    bands = toeplitz(kernels)
    real_band = bands[0]
    imag_band = bands[1]
    table = jnp.stack(
        [jnp.stack([real_band, imag_band], 0), jnp.stack([-imag_band, real_band], 0)], 0
    )
    filtered = jnp.einsum("scbm,cokim->skboi", window, table, preferred_element_type=jnp.float32)
    power = (filtered[:, :, :, 0] ** 2 + filtered[:, :, :, 1] ** 2).astype(jnp.bfloat16)
    quotient = jnp.floor_divide(offsets, count)
    remainder = offsets - quotient * count
    following = passed_along(power, "freq", -1)
    inner = slide(jnp.concatenate([power, following], 2), remainder)
    plane_count = segs * KERNELS
    flat = inner.reshape(plane_count, count * BLOCK)
    plane_quot = quotient.reshape(plane_count)
    distances = lax.broadcasted_iota(jnp.int32, (2 * REACH + 1, plane_count), 0) - REACH
    member = (plane_quot[None, :] == distances).astype(jnp.int32)
    place = jnp.cumsum(member, 1) - 1
    slot_ids = lax.broadcasted_iota(jnp.int32, (2 * REACH + 1, ROUTE_CAP, plane_count), 1)
    select = ((member[:, None, :] == 1) & (place[:, None, :] == slot_ids)).astype(jnp.bfloat16)
    packed = jnp.einsum("dcp,pl->dcl", select, flat, preferred_element_type=jnp.float32).astype(
        jnp.bfloat16
    )
    received = []
    for step_index in range(2 * REACH + 1):
        received.append(passed_along(packed[step_index], "freq", -(step_index - REACH)))
    gathered = jnp.stack(received, 0)
    placed = jnp.einsum("dcp,dcl->pl", select, gathered, preferred_element_type=jnp.float32)
    shifted = placed.astype(jnp.bfloat16).reshape(segs, KERNELS, count, BLOCK)
    levels = lax.broadcasted_iota(jnp.int32, (segs, level_weights.shape[0]), 1)
    weights = jnp.sum(jnp.where(weight_index[:, None] == levels, level_weights[None, :], 0.0), 1)
    scale = 1.0 / (segs * lax.axis_size("seg"))
    partial_sum = jnp.sum((weights * scale)[:, None, None, None] * shifted.astype(jnp.float32), 0)
    owned = lax.psum_scatter(
        partial_sum.astype(jnp.bfloat16), "seg", scatter_dimension=0, tiled=True
    ).astype(jnp.float32)
    return owned.reshape(owned.shape[0], count * BLOCK)


def solution(mesh):
    in_specs = (
        P(("parts", "seg"), None, "freq", None),
        P(),
        P(("parts", "seg"), None),
        P(("parts", "seg")),
        P(),
    )
    out_specs = P(("parts", "seg"), "freq")
    return jax.shard_map(body, mesh=mesh, in_specs=in_specs, out_specs=out_specs, check_vma=False)
```

profile of v0, /device:TPU:0, one launch (start us, length us, event | category | flops | bytes accessed | tf_op | source)
XLA Modules:
  0.0 792.9 jit_solution(5964628973833352408)
XLA Ops:
  8.1 23.1 %fusion.21 = f32[1024,512]{0,1:T(8,128)} fusion(f32[512,1024]{1,0:T(8,128)S(1)} %bitcast.144), kind=kOutput, calls=%fused_computation.37 | convolution fusion | flops 6457131008 | bytes 4194304 | tf_op jit(solution)/shard_map/dot_general | solution.py:68
  31.2 34.4 %fusion.19 = f32[1024,512]{0,1:T(8,128)} fusion(f32[512,1024]{1,0:T(8,128)S(1)} %bitcast.145), kind=kOutput, calls=%fused_computation.35 | convolution fusion | flops 6457131008 | bytes 4194304 | tf_op jit(solution)/shard_map/dot_general | solution.py:69
  72.8 7.3 all-to-all-start
  82.1 23.8 %all-to-all-done = bf16[2,2,128,1024]{2,1,0,3:T(2,128)(2,1)} async-done(((bf16[2,2,128,1024]{2,1,0,3:T(2,128)(2,1)}), bf16[2,2,128,1024]{2,1,0,3:T(2,128)(2,1)}, u32[]{:S(2)}, u32[]{:S(2)}) %all-to-all-start) | async-done | bytes 1048608 | tf_op jit(solution)/shard_map/all_to_all | solution.py:84
  107.3 19.2 %fusion.35 = f32[2,2,128,1024]{3,2,1,0:T(8,128)S(1)} fusion(bf16[2,2,128,8,128]{2,4,3,1,0:T(8,128)(2,1)S(1)} %bitcast.170, s32[8,128]{1,0:T(8,128)S(1)} %multiply_add_fusion), kind=kOutput, calls=%fused_computation.52 | convolution fusion | flops 6457131008 | bytes 3149824 | tf_op jit(solution)/shard_map/scirl,rik->sclk/dot_general | solution.py:92
  126.4 19.3 %fusion.38 = f32[2,2,128,1024]{3,2,1,0:T(8,128)S(1)} fusion(bf16[2,2,128,8,128]{2,4,3,1,0:T(8,128)(2,1)S(1)} %bitcast.171, s32[8,128]{1,0:T(8,128)S(1)} %multiply_add_fusion), kind=kOutput, calls=%fused_computation.53 | convolution fusion | flops 6457131008 | bytes 3149824 | tf_op jit(solution)/shard_map/scirl,rik->sclk/dot_general | solution.py:93
  148.5 3.6 all-to-all-start.1
  153.5 24.5 %all-to-all-done.1 = bf16[2,2,128,1024]{2,1,0,3:T(2,128)(2,1)S(1)} async-done(((bf16[2,2,128,1024]{2,1,0,3:T(2,128)(2,1)}), bf16[2,2,128,1024]{2,1,0,3:T(2,128)(2,1)S(1)}, u32[]{:S(2)}, u32[]{:S(2)}) %all-to-all-start.1) | async-done | bytes 1048608 | tf_op jit(solution)/shard_map/all_to_all | solution.py:97
  181.5 3.3 collective-permute-start.1
  184.8 3.0 maximum_bitcast_fusion.4
  187.8 4.2 pad_maximum_fusion.2
  194.4 6.2 convolution_bitcast_fusion.1
  200.6 3.7 fusion.10
  204.3 3.2 collective-permute-start.2
  208.1 87.3 %collective-permute-done.2 = bf16[2,8,1024,128]{2,3,0,1:T(8,128)(2,1)} collective-permute-done((bf16[2,8,1024,128]{2,3,0,1:T(8,128)(2,1)}, bf16[2,8,1024,128]{2,3,0,1:T(8,128)(2,1)}, u32[]{:S(2)}, u32[]{:S(2)}) %collective-permute-start.2) | collective-permute-done | bytes 4194336 | tf_op jit(solution)/shard_map/ppermute | solution.py:33
  295.4 8.2 %pad_maximum_fusion = bf16[2,8,2048,128]{2,3,0,1:T(8,128)(2,1)} fusion(bf16[2,8,1024,128]{2,3,0,1:T(8,128)(2,1)} %collective-permute-done.2, bf16[2,8,1024,128]{2,3,0,1:T(8,128)(2,1)} %fusion.10), kind=kLoop, calls=%fused_computation.10 | loop fusion | flops 16777216 | bytes 16777216 | tf_op jit(solution)/shard_map/concatenate | solution.py:122
  303.6 71.8 %while.1 = (s32[]{:T(128)}, bf16[2,8,2048,128]{2,3,0,1:T(8,128)(2,1)}, s32[16,4]{0,1:T(4,128)S(1)}, bf16[16,1024,128]{2,1,0:T(8,128)(2,1)}, s32[]{:T(128)}) while((s32[]{:T(128)}, bf16[2,8,2048,128]{2,3,0,1:T(8,128)(2,1)}, s32[16,4]{0,1:T(4,128)S(1)}, bf16[16,1024,128]{2,1,0:T(8,128)(2,1)}, s32[]{:T(128)}) %tuple.54), condition=%wide.while_cond, body=%wide.while_body.sunk | while | flops 2 | bytes 1573509 | solution.py:52
  375.5 4.7 reshape.223
  380.1 10.0 %convolution_convert_fusion = bf16[9,4,131072]{2,0,1:T(8,128)(2,1)} fusion(bf16[16,131072,1]{1,0,2:T(8,128)(2,1)} %reshape.223, s32[9,16]{0,1:T(8,128)S(1)} %copy.202, pred[9,16]{0,1:T(8,128)(4,1)S(1)} %copy.201), kind=kOutput, calls=%fused_computation.3 | convolution fusion | flops 155714688 | bytes 13632208 | tf_op jit(solution)/shard_map/dcp,pl->dcl/dot_general | solution.py:131
  390.2 41.2 %fusion.79 = (bf16[1,4,131072]{2,0,1:T(2,128)(2,1)S(1)}, bf16[1,4,131072]{2,0,1:T(2,128)(2,1)S(1)}, bf16[1,4,131072]{2,0,1:T(2,128)(2,1)}, bf16[1,4,131072]{2,0,...) fusion(bf16[9,4,131072]{2,0,1:T(8,128)(2,1)} %convolution_conve, ...), kind=kLoop, calls=%fused_computation.132 | loop fusion | bytes 18874368 | tf_op jit(solution)/shard_map/slice | solution.py:136
  431.5 3.1 copy.265
  434.6 3.1 copy.264
  437.7 5.6 collective-permute-start.4
  453.9 70.2 %collective-permute-done.3 = bf16[4,131072]{1,0:T(4,128)(2,1)S(1)} collective-permute-done((bf16[4,131072]{1,0:T(4,128)(2,1)S(1)}, bf16[4,131072]{1,0:T(4,128)(2,1)S(1)}, u32[]{:S(2)}, u32[]{:S(2)}) %collective-permute-start.3) | collective-permute-done | bytes 1048608 | tf_op jit(solution)/shard_map/ppermute | solution.py:33
  524.1 47.5 %collective-permute-done.4 = bf16[4,131072]{1,0:T(4,128)(2,1)S(1)} collective-permute-done((bf16[4,131072]{1,0:T(4,128)(2,1)S(1)}, bf16[4,131072]{1,0:T(4,128)(2,1)S(1)}, u32[]{:S(2)}, u32[]{:S(2)}) %collective-permute-start.4) | collective-permute-done | bytes 1048608 | tf_op jit(solution)/shard_map/ppermute | solution.py:33
  572.1 66.9 %collective-permute-start.11 = (bf16[4,131072]{1,0:T(4,128)(2,1)S(1)}, bf16[4,131072]{1,0:T(4,128)(2,1)S(1)}, u32[]{:S(2)}, u32[]{:S(2)}) collective-permute-start(bf16[4,131072]{1,0:T(4,128)(2,1)S(1)} %bitcast.153), channel_id=1, source_target_pairs={{8,0},{10,2},{12,4},{14,6},{0,8},{2,10},{4,12},{6,14},{9,1},{11,3}... | collective-permute-start | bytes 3145736 | tf_op jit(solution)/shard_map/ppermute | solution.py:33
  649.6 3.0 copy.214
  652.6 3.0 copy.215
  655.6 3.2 copy.216
  665.2 74.7 %stack.74 = bf16[9,4,131072]{2,0,1:T(8,128)(2,1)} concatenate(bf16[1,4,131072]{2,0,1:T(2,128)(2,1)S(1)} %copy.210, bf16[1,4,131072]{2,0,1:T(2,128)(2,1)} %copy.211, bf16[1,4,131072]{2,0,1:T(2,128)(2,1)} %copy.212, bf16[1,4,131072]{2,0,1:T(2,128)(2,1)} %copy.213, bf16[1,4,131072]{2,0,1:T(2,128)(2,1)} %copy.214, bf16[1,4,131072]{2,0,1:T(2,128)(2,1)} %copy.215, ...), dimensions={0} | concatenate | bytes 18874368 | tf_op jit(solution)/shard_map/stack | solution.py:137
  739.9 11.0 %fusion.3 = bf16[8,1024,128]{2,0,1:T(8,128)(2,1)S(1)} fusion(f32[2]{0:T(128)S(1)} %broadcast_multiply_fusion, bf16[9,4,131072]{2,0,1:T(8,128)(2,1)} %stack.74, s32[9,16]{0,1:T(8,128)S(1)} %copy.202, pred[9,16]{0,1:T(8,128)(4,1)S(1)} %copy.201), kind=kOutput, calls=%fused_computation.12 | convolution fusion | flops 158336128 | bytes 11535064 | tf_op jit(solution)/shard_map/dcp,dcl->pl/dot_general | solution.py:138
  752.7 29.2 %reduce-scatter.2.cloned.1.call-done = bf16[4,1024,128]{2,1,0:T(8,128)(2,1)} async-done(((bf16[8,1024,128]{2,1,0:T(8,128)(2,1)}), bf16[4,1024,128]{2,1,0:T(8,128)(2,1)}) %reduce-scatter.2.cloned.1.call-update) | async-done | bytes 1048592 | tf_op jit(solution)/shard_map/reduce_scatter | solution.py:144
  (175 shorter events, 127.7 us)
Async XLA Ops:
  6.5 1.6 copy-start
  70.6 9.4 %copy-start.8 = (bf16[2,8,128]{2,1,0:T(8,128)(2,1)S(1)}, bf16[2,8,128]{2,1,0:T(8,128)(2,1)}, u32[]{:S(2)}) copy-start(bf16[2,8,128]{2,1,0:T(8,128)(2,1)} %param.6) | copy-start | bytes 12292
  72.8 33.1 %all-to-all-start = ((bf16[2,2,128,1024]{2,1,0,3:T(2,128)(2,1)}), bf16[2,2,128,1024]{2,1,0,3:T(2,128)(2,1)}, u32[]{:S(2)}, u32[]{:S(2)}) async-start(bf16[2,2,128,1024]{2,1,0,3:T(2,128)(2,1)} %copy.204), calls=%async_computation | async-start | bytes 2097152 | tf_op jit(solution)/shard_map/all_to_all | solution.py:84
  148.5 29.5 %all-to-all-start.1 = ((bf16[2,2,128,1024]{2,1,0,3:T(2,128)(2,1)}), bf16[2,2,128,1024]{2,1,0,3:T(2,128)(2,1)S(1)}, u32[]{:S(2)}, u32[]{:S(2)}) async-start(bf16[2,2,128,1024]{2,1,0,3:T(2,128)(2,1)} %copy.206), calls=%async_computation.1 | async-start | bytes 2097152 | tf_op jit(solution)/shard_map/all_to_all | solution.py:97
  152.0 629.8 %reduce-scatter.2.cloned.1.call-start = ((), (), s32[]{:S(2)}) async-start(), calls=%async_computation.3 | async-start | bytes 3145728 | tf_op jit(solution)/shard_map/reduce_scatter | solution.py:144
  180.0 7.8 collective-permute-start
  181.5 6.3 collective-permute-start.1
  192.0 2.4 copy-start.7
  200.6 6.9 copy-start.9
  204.3 91.2 %collective-permute-start.2 = (bf16[2,8,1024,128]{2,3,0,1:T(8,128)(2,1)}, bf16[2,8,1024,128]{2,3,0,1:T(8,128)(2,1)}, u32[]{:S(2)}, u32[]{:S(2)}) collective-permute-start(bf16[2,8,1024,128]{2,3,0,1:T(8,128)(2,1)} %fusion.10), channel_id=1, source_target_pairs={{2,0},{4,2},{6,4},{8,6},{10,8},{12,10},{14,12},{0,14},{3,1},{5,3},... | collective-permute-start | bytes 12582920 | tf_op jit(solution)/shard_map/ppermute | solution.py:33
  431.4 11.9 %copy-start.6 = (bf16[1,4,131072]{2,0,1:T(2,128)(2,1)S(1)}, bf16[1,4,131072]{2,0,1:T(2,128)(2,1)}, u32[]{:S(2)}) copy-start(bf16[1,4,131072]{2,0,1:T(2,128)(2,1)} %get-tuple-element.92) | copy-start | bytes 3145732
  431.4 13.5 %copy-start.5 = (bf16[1,4,131072]{2,0,1:T(2,128)(2,1)S(1)}, bf16[1,4,131072]{2,0,1:T(2,128)(2,1)}, u32[]{:S(2)}) copy-start(bf16[1,4,131072]{2,0,1:T(2,128)(2,1)} %get-tuple-element.91) | copy-start | bytes 3145732
  434.6 89.6 %collective-permute-start.3 = (bf16[4,131072]{1,0:T(4,128)(2,1)S(1)}, bf16[4,131072]{1,0:T(4,128)(2,1)S(1)}, u32[]{:S(2)}, u32[]{:S(2)}) collective-permute-start(bf16[4,131072]{1,0:T(4,128)(2,1)S(1)} %bitcast.169), channel_id=1, source_target_pairs={{8,0},{10,2},{12,4},{14,6},{0,8},{2,10},{4,12},{6,14},{9,1},{11,3}... | collective-permute-start | bytes 3145736 | tf_op jit(solution)/shard_map/ppermute | solution.py:33
  434.6 12.4 %copy-start.4 = (bf16[1,4,131072]{2,0,1:T(2,128)(2,1)S(1)}, bf16[1,4,131072]{2,0,1:T(2,128)(2,1)}, u32[]{:S(2)}) copy-start(bf16[1,4,131072]{2,0,1:T(2,128)(2,1)} %get-tuple-element.90) | copy-start | bytes 3145732
  437.7 133.9 %collective-permute-start.4 = (bf16[4,131072]{1,0:T(4,128)(2,1)S(1)}, bf16[4,131072]{1,0:T(4,128)(2,1)S(1)}, u32[]{:S(2)}, u32[]{:S(2)}) collective-permute-start(bf16[4,131072]{1,0:T(4,128)(2,1)S(1)} %bitcast.167), channel_id=1, source_target_pairs={{10,0},{12,2},{14,4},{0,6},{2,8},{4,10},{6,12},{8,14},{11,1},{13,3... | collective-permute-start | bytes 3145736 | tf_op jit(solution)/shard_map/ppermute | solution.py:33
  443.4 5.1 copy-start.3
  444.7 126.9 %collective-permute-start.5 = (bf16[4,131072]{1,0:T(4,128)(2,1)S(1)}, bf16[4,131072]{1,0:T(4,128)(2,1)S(1)}, u32[]{:S(2)}, u32[]{:S(2)}) collective-permute-start(bf16[4,131072]{1,0:T(4,128)(2,1)S(1)} %bitcast.165), channel_id=1, source_target_pairs={{12,0},{14,2},{0,4},{2,6},{4,8},{6,10},{8,12},{10,14},{13,1},{15,3... | collective-permute-start | bytes 3145736 | tf_op jit(solution)/shard_map/ppermute | solution.py:33
  445.0 4.8 copy-start.2
  446.4 125.7 %collective-permute-start.6 = (bf16[4,131072]{1,0:T(4,128)(2,1)S(1)}, bf16[4,131072]{1,0:T(4,128)(2,1)S(1)}, u32[]{:S(2)}, u32[]{:S(2)}) collective-permute-start(bf16[4,131072]{1,0:T(4,128)(2,1)S(1)} %bitcast.163), channel_id=1, source_target_pairs={{14,0},{0,2},{2,4},{4,6},{6,8},{8,10},{10,12},{12,14},{15,1},{1,3}... | collective-permute-start | bytes 3145736 | tf_op jit(solution)/shard_map/ppermute | solution.py:33
  448.3 201.3 %collective-permute-start.7 = (bf16[4,131072]{1,0:T(4,128)(2,1)S(1)}, bf16[4,131072]{1,0:T(4,128)(2,1)S(1)}, u32[]{:S(2)}, u32[]{:S(2)}) collective-permute-start(bf16[4,131072]{1,0:T(4,128)(2,1)S(1)} %bitcast.159), channel_id=1, source_target_pairs={{0,0},{2,2},{4,4},{6,6},{8,8},{10,10},{12,12},{14,14},{1,1},{3,3},... | collective-permute-start | bytes 3145736 | tf_op jit(solution)/shard_map/ppermute | solution.py:33
  449.8 189.2 %copy-start.10 = (f32[16]{0:T(128)S(1)}, f32[16]{0:T(128)}, u32[]{:S(2)}) copy-start(f32[16]{0:T(128)} %param.9) | copy-start | bytes 196
  449.8 189.2 %copy-start.11 = (s32[2]{0:T(128)S(1)}, s32[2]{0:T(128)}, u32[]{:S(2)}) copy-start(s32[2]{0:T(128)} %param.8) | copy-start | bytes 28
  524.1 128.5 %collective-permute-start.8 = (bf16[4,131072]{1,0:T(4,128)(2,1)S(1)}, bf16[4,131072]{1,0:T(4,128)(2,1)S(1)}, u32[]{:S(2)}, u32[]{:S(2)}) collective-permute-start(bf16[4,131072]{1,0:T(4,128)(2,1)S(1)} %bitcast.161), channel_id=1, source_target_pairs={{2,0},{4,2},{6,4},{8,6},{10,8},{12,10},{14,12},{0,14},{3,1},{5,3},... | collective-permute-start | bytes 3145736 | tf_op jit(solution)/shard_map/ppermute | solution.py:33
  571.6 84.0 %collective-permute-start.9 = (bf16[4,131072]{1,0:T(4,128)(2,1)S(1)}, bf16[4,131072]{1,0:T(4,128)(2,1)S(1)}, u32[]{:S(2)}, u32[]{:S(2)}) collective-permute-start(bf16[4,131072]{1,0:T(4,128)(2,1)S(1)} %bitcast.157), channel_id=1, source_target_pairs={{4,0},{6,2},{8,4},{10,6},{12,8},{14,10},{0,12},{2,14},{5,1},{7,3},... | collective-permute-start | bytes 3145736 | tf_op jit(solution)/shard_map/ppermute | solution.py:33
  571.7 87.1 %collective-permute-start.10 = (bf16[4,131072]{1,0:T(4,128)(2,1)S(1)}, bf16[4,131072]{1,0:T(4,128)(2,1)S(1)}, u32[]{:S(2)}, u32[]{:S(2)}) collective-permute-start(bf16[4,131072]{1,0:T(4,128)(2,1)S(1)} %bitcast.155), channel_id=1, source_target_pairs={{6,0},{8,2},{10,4},{12,6},{14,8},{0,10},{2,12},{4,14},{7,1},{9,3},... | collective-permute-start | bytes 3145736 | tf_op jit(solution)/shard_map/ppermute | solution.py:33
  572.1 90.2 %collective-permute-start.11 = (bf16[4,131072]{1,0:T(4,128)(2,1)S(1)}, bf16[4,131072]{1,0:T(4,128)(2,1)S(1)}, u32[]{:S(2)}, u32[]{:S(2)}) collective-permute-start(bf16[4,131072]{1,0:T(4,128)(2,1)S(1)} %bitcast.153), channel_id=1, source_target_pairs={{8,0},{10,2},{12,4},{14,6},{0,8},{2,10},{4,12},{6,14},{9,1},{11,3}... | collective-permute-start | bytes 3145736 | tf_op jit(solution)/shard_map/ppermute | solution.py:33
  752.6 33.3 %copy-start.1 = (f32[2,2,128,1024]{3,2,1,0:T(8,128)S(1)}, f32[2,2,128,1024]{3,2,1,0:T(8,128)}, u32[]{:S(2)}) copy-start(f32[2,2,128,1024]{3,2,1,0:T(8,128)} %param.5) | copy-start | bytes 6291460
Sparse Core Ops, SparseCore 0:
  752.8 29.0 reduce-scatter.1
where the time goes:
time: 806 us; the launch traced here: 793 us
  waiting for transfers between devices  283 us (35%)
  local copies, waits for them, and re-layouts  251 us (31%)
  matrix products  123 us (15%)
  starting transfers between devices  92.8 us (12%)
  other arithmetic  28.8 us (4%)
  between operations  14 us (2%)
    ppermute x10, waiting for transfers between devices, passed_along(): return lax.ppermute(block, axis, route)  206 us
    another operation x10, local copies, waits for them, and re-layouts, body(): gathered = jnp.stack(received, 0)  100 us
    ppermute x10, starting transfers between devices, passed_along(): return lax.ppermute(block, axis, route)  77.1 us
    gather x80, local copies, waits for them, and re-layouts  71.4 us
    slice x1, local copies, waits for them, and re-layouts, body(): packed[step_index]  41.2 us
    dot_general x1, matrix products, body(): jnp.dot(stacked, sin_two, precision=highest).reshape(samples.shape)  34.4 us
    reduce_scatter x1, waiting for transfers between devices, body(): lax.psum_scatter(partial_sum.astype(jnp.bfloat16), 'seg', scatter_dimensi...  29.2 us
    all_to_all x1, waiting for transfers between devices, body(): lax.all_to_all(second.astype(jnp.bfloat16), 'freq', split_axis=3, concat_...  24.5 us
  transfers between devices with their start and end apart: 15, of which 7 were waited for; matrix products, arithmetic and copies ran while one was open for 5% of the time, Pallas kernels for 0%

commit v1 on v0

--- a/solution.py
+++ b/solution.py
@@ -1,8 +1,13 @@
 import math
+
+import functools
 
 import jax
 import jax.numpy as jnp
+import numpy as np
 from jax import lax
+from jax.experimental import pallas as pl
+from jax.experimental.pallas import tpu as pltpu
 from jax.sharding import PartitionSpec as P
 
 BLOCK = 128
@@ -56,7 +61,7 @@
     return jax.vmap(jax.vmap(take_blocks))(joined, starts)
 
 
-def body(samples, kernels, offsets, weight_index, level_weights):
+def general(samples, kernels, offsets, weight_index, level_weights):
     segs, comps, rows_one, cols_two = samples.shape
     ranks = lax.axis_size("freq")
     here = lax.axis_index("freq")
@@ -147,6 +152,228 @@
     return owned.reshape(owned.shape[0], count * BLOCK)
 
 
+VMEM = pl.BlockSpec(memory_space=pltpu.VMEM)
+SMEM = pl.BlockSpec(memory_space=pltpu.SMEM)
+PAD = 16
+BF16 = jnp.bfloat16
+F32 = jnp.float32
+
+
+def unit(turns, scale=1.0):
+    angle = 2.0 * np.pi * turns
+    return (np.cos(angle) * scale).astype(np.float32), (np.sin(angle) * scale).astype(np.float32)
+
+
+def wave_bases(size, first):
+    step = math.isqrt(size)
+    while size % step:
+        step -= 1
+    cols = np.arange(size) + first
+    low = np.arange(step)[:, None] * cols[None, :] % size / size
+    high = np.arange(size // step)[:, None] * step * cols[None, :] % size / size
+    return unit(low) + unit(high)
+
+
+def fill_waves(low_cos, low_sin, high_cos, high_sin, cos_ref, sin_ref):
+    step = low_cos.shape[0]
+
+    @pl.loop(0, high_cos.shape[0])
+    def _(i):
+        hc = high_cos[pl.ds(i, 1), :]
+        hs = high_sin[pl.ds(i, 1), :]
+        lc = low_cos[...]
+        ls = low_sin[...]
+        rows = pl.ds(pl.multiple_of(i * step, step), step)
+        cos_ref[rows, :] = (hc * lc - hs * ls).astype(BF16)
+        sin_ref[rows, :] = (hs * lc + hc * ls).astype(BF16)
+
+
+def first_kernel(x_ref, lc, ls, hc, hs, tc, ts, dc, ds_, out_ref, cos_ref, sin_ref, xb_ref, far_ref):
+    segs, comps, rows, cols = x_ref.shape
+    here = lax.axis_index("freq")
+    fill_waves(lc, ls, hc, hs, cos_ref, sin_ref)
+    far_ref[0:1, :] = dc[pl.ds(here, 1), :]
+    far_ref[8:9, :] = ds_[pl.ds(here, 1), :]
+    for s in range(segs):
+        for c in range(comps):
+            at = (s * comps + c) * rows
+            xb_ref[at : at + rows, :] = x_ref[s, c].astype(BF16)
+
+    @pl.loop(0, out_ref.shape[0])
+    def _(j):
+        lanes = pl.ds(pl.multiple_of(j * BLOCK, BLOCK), BLOCK)
+        rhs = jnp.concatenate([cos_ref[:, lanes], sin_ref[:, lanes]], 1)
+        got = jnp.dot(xb_ref[...], rhs, preferred_element_type=F32)
+        a = far_ref[0:1, lanes]
+        b = far_ref[8:9, lanes]
+        wc = a * tc[:, lanes] - b * ts[:, lanes]
+        ws = b * tc[:, lanes] + a * ts[:, lanes]
+        for s in range(segs):
+            top = got[2 * s * rows : (2 * s + 1) * rows]
+            bottom = got[(2 * s + 1) * rows : (2 * s + 2) * rows]
+            re = top[:, :BLOCK] + bottom[:, BLOCK:]
+            im = bottom[:, :BLOCK] - top[:, BLOCK:]
+            out_ref[j, s, 0] = (re * wc + im * ws).astype(BF16)
+            out_ref[j, s, 1] = (im * wc - re * ws).astype(BF16)
+
+
+def second_kernel(x_ref, lc, ls, hc, hs, out_ref, cos_ref, sin_ref, rhs_ref):
+    ranks, segs, comps, rows, width = x_ref.shape
+    fill_waves(lc, ls, hc, hs, cos_ref, sin_ref)
+    for d in range(ranks):
+        for s in range(segs):
+            for c in range(comps):
+                at = (s * comps + c) * width
+                rhs_ref[d * rows : (d + 1) * rows, at : at + width] = x_ref[d, s, c]
+
+    @pl.loop(0, ranks)
+    def _(i):
+        here = pl.ds(pl.multiple_of(i * rows, rows), rows)
+        yc = jnp.dot(cos_ref[here, :], rhs_ref[...], preferred_element_type=F32)
+        ys = jnp.dot(sin_ref[here, :], rhs_ref[...], preferred_element_type=F32)
+        for s in range(segs):
+            re, im = 2 * s * width, (2 * s + 1) * width
+            out_ref[s, 0, here] = (yc[:, re : re + width] + ys[:, im : im + width]).astype(BF16)
+            out_ref[s, 1, here] = (yc[:, im : im + width] - ys[:, re : re + width]).astype(BF16)
+
+
+def fill_bands(u_ref, band_ref):
+    wide = 2 * BLOCK
+
+    @pl.loop(0, u_ref.shape[1])
+    def _(t):
+        both = []
+        for c in range(2):
+            row = jnp.broadcast_to(u_ref[c, pl.ds(t, 1), :], (wide, wide))
+            both.append(pltpu.roll(row, 0, 1, stride=1, stride_axis=0)[:, :BLOCK])
+        re, im = both
+        band_ref[t, :wide, :BLOCK] = re.astype(BF16)
+        band_ref[t, :wide, BLOCK:] = im.astype(BF16)
+        band_ref[t, wide:, :BLOCK] = (-im).astype(BF16)
+        band_ref[t, wide:, BLOCK:] = re.astype(BF16)
+
+
+def filter_one(w_ref, band_ref, p_ref, off_ref, s, t, rows, ranks):
+    total = w_ref.shape[3] - rows - PAD
+    here = lax.axis_index("freq")
+    blocks = total * ranks
+    base = lax.rem(here * rows * ranks + off_ref[s, t] + blocks, blocks)
+    gk = base // ranks
+    gj = base - gk * ranks
+    tall = rows + PAD
+    parts = []
+    shifts = []
+    for jj in range(ranks):
+        jv = gj + jj
+        carry = (jv >= ranks).astype(jnp.int32)
+        j = jv - carry * ranks
+        row = lax.rem(gk + carry, total)
+        low = row // PAD * PAD
+        shifts.append(row - low)
+        take = pl.ds(pl.multiple_of(low, PAD), tall)
+        parts.append(
+            jnp.concatenate(
+                [w_ref[s, 0, j, take, :], w_ref[s, 0, j + 1, take, :], w_ref[s, 1, j, take, :], w_ref[s, 1, j + 1, take, :]],
+                1,
+            )
+        )
+    got = jnp.dot(jnp.concatenate(parts, 0), band_ref[t], preferred_element_type=F32)
+    re = got[:, :BLOCK]
+    im = got[:, BLOCK:]
+    p_ref[...] = re * re + im * im
+    return [p_ref[pl.ds(jj * tall + shifts[jj], rows), :] for jj in range(ranks)]
+
+
+def filter_kernel(off_ref, wi_ref, lw_ref, g_ref, u_ref, mine_ref, other_ref, w_ref, band_ref, p_ref):
+    ranks, segs, comps, total, width = g_ref.shape
+    rows = total // ranks
+    scale = 1.0 / (segs * 2)
+    core = lax.axis_index("seg")
+    fill_bands(u_ref, band_ref)
+    for s in range(segs):
+        for c in range(comps):
+            for j in range(ranks):
+                w_ref[s, c, j, :total] = g_ref[j, s, c]
+                w_ref[s, c, j, total:] = g_ref[j, s, c, : rows + PAD]
+            x = g_ref[0, s, c].astype(F32)
+            x = jnp.concatenate([x[1:], x[:1]], 0).astype(BF16)
+            w_ref[s, c, ranks, :total] = x
+            w_ref[s, c, ranks, total:] = x[: rows + PAD]
+    half = mine_ref.shape[0]
+    weights = [lw_ref[wi_ref[s]] * scale for s in range(segs)]
+    for out_ref, first in ((other_ref, (1 - core) * half), (mine_ref, core * half)):
+
+        @pl.loop(0, half)
+        def _(i):
+            sums = None
+            for s in range(segs):
+                got = filter_one(w_ref, band_ref, p_ref.at[s], off_ref, s, first + i, rows, ranks)
+                got = [weights[s] * x for x in got]
+                sums = got if sums is None else [x + y for x, y in zip(sums, got)]
+            for jj in range(ranks):
+                out_ref[i, :, jj * BLOCK : (jj + 1) * BLOCK] = sums[jj].astype(out_ref.dtype)
+
+
+def reversed_taps(kernels):
+    k = kernels.astype(F32)
+    zeros = jnp.zeros(k.shape[:-1] + (k.shape[-1],), F32)
+    return jnp.concatenate([k[..., :1], zeros, jnp.flip(k[..., 1:], -1)], -1)
+
+
+def params(**more):
+    return pltpu.CompilerParams(vmem_limit_bytes=60 << 20, **more)
+
+
+def body(samples, kernels, offsets, weight_index, level_weights):
+    segs, comps, rows, cols = samples.shape
+    ranks = lax.axis_size("freq")
+    size_one = rows * ranks
+    if cols != ranks * BLOCK or rows != BLOCK or lax.axis_size("seg") != 2:
+        return general(samples, kernels, offsets, weight_index, level_weights)
+    length = size_one * cols
+    bins = np.arange(cols) - BLOCK // 2
+    near = unit(np.arange(rows)[:, None] * bins[None, :] % length / length, 1.0 / math.sqrt(length))
+    far = unit(np.arange(ranks)[:, None] * rows * bins[None, :] % length / length)
+    turned = pl.pallas_call(
+        first_kernel,
+        out_shape=jax.ShapeDtypeStruct((ranks, segs, comps, rows, BLOCK), BF16),
+        in_specs=[VMEM] * 9,
+        out_specs=VMEM,
+        scratch_shapes=[pltpu.VMEM((cols, cols), BF16)] * 2 + [pltpu.VMEM((segs * comps * rows, cols), BF16), pltpu.VMEM((16, cols), F32)],
+        compiler_params=params(),
+    )(samples, *wave_bases(cols, -(BLOCK // 2)), *near, *far)
+    arrived = lax.all_to_all(turned, "freq", split_axis=0, concat_axis=0, tiled=True)
+    spectrum = pl.pallas_call(
+        second_kernel,
+        out_shape=jax.ShapeDtypeStruct((segs, comps, size_one, BLOCK), BF16),
+        in_specs=[VMEM] * 5,
+        out_specs=VMEM,
+        scratch_shapes=[pltpu.VMEM((size_one, size_one), BF16)] * 2
+        + [pltpu.VMEM((size_one, segs * comps * BLOCK), BF16)],
+        compiler_params=params(),
+    )(arrived, *wave_bases(size_one, 0))
+    gathered = lax.all_gather(spectrum, "freq", axis=0)
+    half = kernels.shape[1] // 2
+    tall = rows + PAD
+    mine, other = pl.pallas_call(
+        filter_kernel,
+        out_shape=(
+            jax.ShapeDtypeStruct((half, rows, cols), F32),
+            jax.ShapeDtypeStruct((half, rows, cols), BF16),
+        ),
+        in_specs=[SMEM] * 3 + [VMEM] * 2,
+        out_specs=(VMEM, VMEM),
+        scratch_shapes=[
+            pltpu.VMEM((segs, comps, ranks + 1, size_one + tall, BLOCK), BF16),
+            pltpu.VMEM((kernels.shape[1], 4 * BLOCK, 2 * BLOCK), BF16),
+            pltpu.VMEM((segs, ranks * tall, BLOCK), F32),
+        ],
+        compiler_params=params(),
+    )(offsets, weight_index, level_weights, gathered, reversed_taps(kernels))
+    swapped = lax.ppermute(other, "seg", [(0, 1), (1, 0)])
+    return (mine + swapped.astype(F32)).reshape(half, rows * cols)
+
+
 def solution(mesh):
     in_specs = (
         P(("parts", "seg"), None, "freq", None),

time: 806 us -> 209 us (0.26); the launches traced: 793 us -> 208 us
  local copies, waits for them, and re-layouts: 251 us -> 2.9 us
  waiting for transfers between devices: 283 us -> 126 us
  matrix products: 123 us -> 0 us
  starting transfers between devices: 92.8 us -> 0.01 us
  blocking collectives: 0 us -> 33.1 us
  Pallas kernels: 0 us -> 30.7 us
  other arithmetic: 28.8 us -> 2.61 us
    ppermute x12 -> x1, waiting for transfers between devices: 206 us -> 2.87 us  [body(): swapped = lax.ppermute(other, 'seg', [(0, 1), (1, 0)])]
    dot_general x7 -> x0, matrix products: 123 us -> none  [the longest x1 34.4 us: body(): jnp.dot(stacked, sin_two, precision=highest).reshape(samples.shape)]
    all_gather x0 -> x1, waiting for transfers between devices: none -> 123 us  [body(): gathered = lax.all_gather(spectrum, 'freq', axis=0)]
    another operation x14 -> x0, local copies, waits for them, and re-layouts: 106 us -> none  [the longest x10 100 us: body(): gathered = jnp.stack(received, 0)]
    ppermute x12 -> x1, starting transfers between devices: 81.9 us -> 0.01 us  [body(): swapped = lax.ppermute(other, 'seg', [(0, 1), (1, 0)])]
    gather x81 -> x0, local copies, waits for them, and re-layouts: 71.5 us -> none
    all_to_all x2 -> x0, waiting for transfers between devices: 48.4 us -> none  [the longest x1 24.5 us: body(): lax.all_to_all(second.astype(jnp.bfloat16), 'freq', split_axis=3, concat_...]
    slice x3 -> x2, local copies, waits for them, and re-layouts: 41.4 us -> 0.08 us  [reversed_taps(): return jnp.concatenate([k[..., :1], zeros, jnp.flip(k[..., 1:], -1)], -1)]
  transfers between devices with their start and end apart: 15 -> 2, of which waited for: 7 -> 2; matrix products, arithmetic and copies ran while one was open for 5% -> 0% of each run, Pallas kernels for 0% -> 0%
where the time goes in v1:
time: 209 us; the launch traced here: 208 us
  waiting for transfers between devices  126 us (60%)
  blocking collectives  33.1 us (16%)
  Pallas kernels  30.7 us (15%)
  between operations  13.4 us (6%)
  local copies, waits for them, and re-layouts  2.9 us (1%)
  other arithmetic  2.61 us (1%)
    all_gather x1, waiting for transfers between devices, body(): gathered = lax.all_gather(spectrum, 'freq', axis=0)  123 us
    all_to_all x1, blocking collectives, body(): lax.all_to_all(turned, 'freq', split_axis=0, concat_axis=0, tiled=True)  33.1 us
    pallas_call x1, Pallas kernels, body(): pl.pallas_call(filter_kernel, out_shape=(jax.ShapeDtypeStruct((half, rows...  14.7 us
    pallas_call x1, Pallas kernels, body(): pl.pallas_call(first_kernel, out_shape=jax.ShapeDtypeStruct((ranks, segs,...  8.49 us
    pallas_call x1, Pallas kernels, body(): pl.pallas_call(second_kernel, out_shape=jax.ShapeDtypeStruct((segs, comps...  7.5 us
  transfers between devices with their start and end apart: 2, of which 2 were waited for; matrix products, arithmetic and copies ran while one was open for 0% of the time, Pallas kernels for 0%

profile of v1, /device:TPU:0, one launch (start us, length us, event | category | flops | bytes accessed | tf_op | source)
XLA Modules:
  0.0 208.4 jit_solution(14649834614848028119)
XLA Ops:
  6.5 0.0 all-gather.3.cloned.1.call-start
  6.5 8.5 %shard_map.163 = bf16[8,2,2,128,128]{4,3,2,1,0:T(8,128)(2,1)} custom-call(f32[2,2,128,1024]{3,2,1,0:T(8,128)} %x_ref.1, f32[32,1024]{1,0:T(8,128)} %constant.22.clone.lc, f32[32,1024]{1,0:T(8,128)} %constant.23.clone.ls, f32[32,1024]{1,0:T(8,128)} %constant.24.clone.hc, f32[32,1024]{1,0:T(8,128)} %constant.25.clone.hs, f32[128,1024]{1,0:T(8,128)} %constant.26.clone.tc, ...), custom_call_target="tpu_custom_call" | custom-call | tf_op jit(solution)/shard_map/pallas_call | solution.py:337
  15.0 33.1 %all_to_all.5.x_ref = bf16[8,2,2,128,128]{4,3,2,1,0:T(8,128)(2,1)} all-to-all(bf16[8,2,2,128,128]{4,3,2,1,0:T(8,128)(2,1)} %shard_map.163), channel_id=1, replica_groups=mesh['parts'=2,'freq'=8,'seg'=2] {'freq'}, dimensions={0} | all-to-all | bytes 2097152 | tf_op jit(solution)/shard_map/all_to_all | solution.py:345
  48.2 0.0 copy-start
  48.2 7.5 %shard_map.164 = bf16[2,2,1024,128]{3,2,1,0:T(8,128)(2,1)} custom-call(bf16[8,2,2,128,128]{4,3,2,1,0:T(8,128)(2,1)} %all_to_all.5.x_ref, f32[32,1024]{1,0:T(8,128)} %constant.30.clone.lc, f32[32,1024]{1,0:T(8,128)} %constant.31.clone.ls, f32[32,1024]{1,0:T(8,128)} %constant.24.clone.hc, f32[32,1024]{1,0:T(8,128)} %constant.25.clone.hs), custom_call_target="tpu_custom_call" | custom-call | tf_op jit(solution)/shard_map/pallas_call | solution.py:346
  55.7 0.0 all-gather.3.cloned.1.call-update
  55.7 0.0 copy-done
  55.7 0.1 slice.9
  55.8 0.1 rev.4
  55.9 0.1 pad.1.clone
  55.9 0.7 pad_maximum_fusion.u_ref
  56.6 122.7 %all-gather.3.cloned.1.call-done = bf16[16,2,1024,128]{3,2,1,0:T(8,128)(2,1)} async-done(((bf16[2,2,1024,128]{3,2,1,0:T(8,128)(2,1)}), bf16[16,2,1024,128]{3,2,1,0:T(8,128)(2,1)}) %all-gather.3.cloned.1.call-update) | async-done | bytes 8388624 | tf_op jit(solution)/shard_map/all_gather | solution.py:355
  179.4 14.7 %shard_map.165 = (f32[4,128,1024]{2,1,0:T(8,128)}, bf16[4,128,1024]{2,1,0:T(8,128)(2,1)}) custom-call(s32[2,8]{1,0:T(2,128)} %off_ref.1, s32[2]{0:T(128)} %wi_ref.1, f32[16]{0:T(128)} %lw_ref.1, bf16[8,2,2,1024,128]{4,3,2,1,0:T(8,128)(2,1)} %bitcast.4, f32[2,8,256]{2,1,0:T(8,128)} %pad_maximum_fusion.u_ref), custom_call_target="tpu_custom_call" | custom-call | tf_op jit(solution)/shard_map/pallas_call | solution.py:358
  194.1 0.0 collective-permute-start
  194.1 2.9 %collective-permute-done = bf16[4,128,1024]{2,1,0:T(8,128)(2,1)S(1)} collective-permute-done((bf16[4,128,1024]{2,1,0:T(8,128)(2,1)}, bf16[4,128,1024]{2,1,0:T(8,128)(2,1)S(1)}, u32[]{:S(2)}, u32[]{:S(2)}) %collective-permute-start) | collective-permute-done | bytes 1048608 | tf_op jit(solution)/shard_map/ppermute | solution.py:373
  197.0 1.9 add_bitcast_fusion
  198.9 2.7 %copy.18 = f32[1,4,128,1024]{3,1,2,0:T(4,128)} copy(f32[1,4,128,1024]{3,2,1,0:T(8,128)S(1)} %add_bitcast_fusion) | data formatting | bytes 4194304
  (2 shorter events, 0.0 us)
Async XLA Ops:
  6.5 172.8 %all-gather.3.cloned.1.call-start = ((), (), s32[]{:S(2)}) async-start(), calls=%async_computation.1 | async-start | bytes 9437184 | tf_op jit(solution)/shard_map/all_gather | solution.py:355
  48.2 7.5 %copy-start = (bf16[2,8,128]{2,1,0:T(8,128)(2,1)S(1)}, bf16[2,8,128]{2,1,0:T(8,128)(2,1)}, u32[]{:S(2)}) copy-start(bf16[2,8,128]{2,1,0:T(8,128)(2,1)} %param.18) | copy-start | bytes 12292
  194.1 2.9 %collective-permute-start = (bf16[4,128,1024]{2,1,0:T(8,128)(2,1)}, bf16[4,128,1024]{2,1,0:T(8,128)(2,1)S(1)}, u32[]{:S(2)}, u32[]{:S(2)}) collective-permute-start(bf16[4,128,1024]{2,1,0:T(8,128)(2,1)} %get-tuple-element.8), channel_id=1, source_target_pairs={{0,1},{1,0},{2,3},{3,2},{4,5},{5,4},{6,7},{7,6},{8,9},{9,8},{10,11... | collective-permute-start | bytes 3145736 | tf_op jit(solution)/shard_map/ppermute | solution.py:373
Sparse Core Ops, SparseCore 0:
  55.8 123.4 all-gather.2

commit v2 on v0

--- a/solution.py
+++ b/solution.py
@@ -1,8 +1,13 @@
 import math
+
+import functools
 
 import jax
 import jax.numpy as jnp
+import numpy as np
 from jax import lax
+from jax.experimental import pallas as pl
+from jax.experimental.pallas import tpu as pltpu
 from jax.sharding import PartitionSpec as P
 
 BLOCK = 128
@@ -56,7 +61,7 @@
     return jax.vmap(jax.vmap(take_blocks))(joined, starts)
 
 
-def body(samples, kernels, offsets, weight_index, level_weights):
+def general(samples, kernels, offsets, weight_index, level_weights):
     segs, comps, rows_one, cols_two = samples.shape
     ranks = lax.axis_size("freq")
     here = lax.axis_index("freq")
@@ -147,6 +152,306 @@
     return owned.reshape(owned.shape[0], count * BLOCK)
 
 
+VMEM = pl.BlockSpec(memory_space=pltpu.VMEM)
+SMEM = pl.BlockSpec(memory_space=pltpu.SMEM)
+PAD = 16
+BF16 = jnp.bfloat16
+F32 = jnp.float32
+
+
+def unit(turns, scale=1.0):
+    angle = 2.0 * np.pi * turns
+    return (np.cos(angle) * scale).astype(np.float32), (np.sin(angle) * scale).astype(np.float32)
+
+
+def wave_bases(size, first):
+    step = math.isqrt(size)
+    while size % step:
+        step -= 1
+    cols = np.arange(size) + first
+    low = np.arange(step)[:, None] * cols[None, :] % size / size
+    high = np.arange(size // step)[:, None] * step * cols[None, :] % size / size
+    return unit(low) + unit(high)
+
+
+def fill_waves(low_cos, low_sin, high_cos, high_sin, cos_ref, sin_ref):
+    step = low_cos.shape[0]
+
+    @pl.loop(0, high_cos.shape[0])
+    def _(i):
+        hc = high_cos[pl.ds(i, 1), :]
+        hs = high_sin[pl.ds(i, 1), :]
+        lc = low_cos[...]
+        ls = low_sin[...]
+        rows = pl.ds(pl.multiple_of(i * step, step), step)
+        cos_ref[rows, :] = (hc * lc - hs * ls).astype(BF16)
+        sin_ref[rows, :] = (hs * lc + hc * ls).astype(BF16)
+
+
+def fill_bands(u_ref, band_ref):
+    wide = 2 * BLOCK
+
+    @pl.loop(0, u_ref.shape[1])
+    def _(t):
+        both = []
+        for c in range(2):
+            row = jnp.broadcast_to(u_ref[c, pl.ds(t, 1), :], (wide, wide))
+            both.append(pltpu.roll(row, 0, 1, stride=1, stride_axis=0)[:, :BLOCK])
+        re, im = both
+        band_ref[t, :wide, :BLOCK] = re.astype(BF16)
+        band_ref[t, :wide, BLOCK:] = im.astype(BF16)
+        band_ref[t, wide:, :BLOCK] = (-im).astype(BF16)
+        band_ref[t, wide:, BLOCK:] = re.astype(BF16)
+
+
+def remote(src, dst, sems, at, axis, device):
+    return pltpu.make_async_remote_copy(
+        src_ref=src,
+        dst_ref=dst,
+        send_sem=sems[0].at[at],
+        recv_sem=sems[1].at[at],
+        device_id={axis: device},
+        device_id_type=pl.DeviceIdType.MESH,
+    )
+
+
+def first_step(s, x_ref, cos_ref, sin_ref, xb_ref, near_cos, near_sin, far_ref, j):
+    rows = x_ref.shape[2]
+    lanes = pl.ds(pl.multiple_of(j * BLOCK, BLOCK), BLOCK)
+    rhs = jnp.concatenate([cos_ref[:, lanes], sin_ref[:, lanes]], 1)
+    got = jnp.dot(xb_ref[s], rhs, preferred_element_type=F32)
+    a = far_ref[0:1, lanes]
+    b = far_ref[8:9, lanes]
+    wc = a * near_cos[:, lanes] - b * near_sin[:, lanes]
+    ws = b * near_cos[:, lanes] + a * near_sin[:, lanes]
+    re = got[:rows, :BLOCK] + got[rows:, BLOCK:]
+    im = got[rows:, :BLOCK] - got[:rows, BLOCK:]
+    return jnp.concatenate([re * wc + im * ws, im * wc - re * ws], 1).astype(BF16)
+
+
+def second_step(s, cos_ref, sin_ref, rhs_ref, w_ref, me, ranks):
+    rows = cos_ref.shape[0] // ranks
+
+    @pl.loop(0, ranks)
+    def _(i):
+        here = pl.ds(pl.multiple_of(i * rows, rows), rows)
+        yc = jnp.dot(cos_ref[here, :], rhs_ref[s], preferred_element_type=F32)
+        ys = jnp.dot(sin_ref[here, :], rhs_ref[s], preferred_element_type=F32)
+        w_ref[0, me, here, :] = (yc[:, :BLOCK] + ys[:, BLOCK:]).astype(BF16)
+        w_ref[1, me, here, :] = (yc[:, BLOCK:] - ys[:, :BLOCK]).astype(BF16)
+
+
+def pad_edges(w_ref, total, ranks):
+    tall = w_ref.shape[2] - total
+    for c in range(2):
+        x = w_ref[c, 0, :total, :].astype(F32)
+        w_ref[c, ranks, :total, :] = jnp.concatenate([x[1:], x[:1]], 0).astype(BF16)
+        for j in range(ranks + 1):
+            w_ref[c, j, total:, :] = w_ref[c, j, :tall, :]
+
+
+def filter_one(w_ref, band_ref, p_ref, off_ref, s, t, rows, ranks):
+    total = rows * ranks
+    here = lax.axis_index("freq")
+    blocks = total * ranks
+    base = lax.rem(here * total + off_ref[s, t] + blocks, blocks)
+    gk = base // ranks
+    gj = base - gk * ranks
+    tall = rows + PAD
+    parts = []
+    shifts = []
+    for jj in range(ranks):
+        carry = (gj + jj) // ranks
+        j = gj + jj - carry * ranks
+        row = lax.rem(gk + carry, total)
+        low = row // PAD * PAD
+        shifts.append(row - low)
+        take = pl.ds(pl.multiple_of(low, PAD), tall)
+        pieces = [w_ref[0, j, take, :], w_ref[0, j + 1, take, :], w_ref[1, j, take, :], w_ref[1, j + 1, take, :]]
+        parts.append(jnp.concatenate(pieces, 1))
+    got = jnp.dot(jnp.concatenate(parts, 0), band_ref[t], preferred_element_type=F32)
+    re = got[:, :BLOCK]
+    im = got[:, BLOCK:]
+    p_ref[...] = re * re + im * im
+    return [p_ref[pl.ds(jj * tall + shifts[jj], rows), :] for jj in range(ranks)]
+
+
+def gather_kernel(
+    x_ref, u_ref,
+    b_lc, b_ls, b_hc, b_hs, e_lc, e_ls, e_hc, e_hs, near_cos, near_sin, far_cos, far_sin,
+    w_first, w_second, band_ref,
+    cos_ref, sin_ref, xb_ref, far_ref, turned, rhs_ref,
+    ex_send, ex_recv, up_send, up_recv, down_send, down_recv,
+):
+    segs, comps, rows, cols = x_ref.shape
+    ranks = lax.axis_size("freq")
+    total = rows * ranks
+    me = lax.axis_index("freq")
+    w_refs = (w_first, w_second)
+    exchange = (ex_send, ex_recv)
+
+    barrier = pltpu.get_barrier_semaphore()
+    for d in range(1, ranks):
+        peer = (me + d) % ranks
+        pl.semaphore_signal(barrier, inc=1, device_id={"freq": peer}, device_id_type=pl.DeviceIdType.MESH)
+    pl.semaphore_wait(barrier, ranks - 1)
+
+    fill_waves(b_lc, b_ls, b_hc, b_hs, cos_ref, sin_ref)
+    far_ref[0:1, :] = far_cos[pl.ds(me, 1), :]
+    far_ref[8:9, :] = far_sin[pl.ds(me, 1), :]
+    for s in range(segs):
+        for c in range(comps):
+            xb_ref[s, c * rows : (c + 1) * rows, :] = x_ref[s, c].astype(BF16)
+
+    def sent(s, d):
+        here = pl.ds(pl.multiple_of(me * rows, rows), rows)
+        return remote(turned.at[s, d], rhs_ref.at[s, here, :], exchange, (s, d), "freq", (me + d) % ranks)
+
+    def own_rows():
+        return pl.ds(pl.multiple_of(me * rows, rows), rows)
+
+    for s in range(segs):
+        step = functools.partial(first_step, s, x_ref, cos_ref, sin_ref, xb_ref, near_cos, near_sin, far_ref)
+
+        @pl.loop(1, ranks)
+        def _(d):
+            turned[s, d] = step((me + d) % ranks)
+            sent(s, d).start()
+
+        rhs_ref[s, own_rows(), :] = step(me)
+
+    fill_waves(e_lc, e_ls, e_hc, e_hs, cos_ref, sin_ref)
+    fill_bands(u_ref, band_ref)
+
+    odd = me % 2
+    place = (1 - odd) * (me // 2) + odd * (ranks - 1 - me // 2)
+
+    def at_place(p):
+        p = (p + ranks) % ranks
+        far = p // (ranks // 2)
+        return (1 - far) * (2 * p) + far * (2 * (ranks - 1 - p) + 1)
+
+    mid = total // 2
+
+    def hop(s, c, k, way):
+        owner = at_place(place - k) if way == 0 else at_place(place + k)
+        target = at_place(place + 1) if way == 0 else at_place(place - 1)
+        block = w_refs[s].at[c, owner, pl.ds(way * mid, mid), :]
+        sems = ((up_send, up_recv), (down_send, down_recv))[way]
+        return remote(block, block, sems, (s, c, k), "freq", target)
+
+    def landed(s, c, k, way):
+        owner = at_place(place - k - 1) if way == 0 else at_place(place + k + 1)
+        target = at_place(place + 1) if way == 0 else at_place(place - 1)
+        block = w_refs[s].at[c, owner, pl.ds(way * mid, mid), :]
+        sems = ((up_send, up_recv), (down_send, down_recv))[way]
+        return remote(block, block, sems, (s, c, k), "freq", target)
+
+    for s in range(segs):
+        for d in range(1, ranks):
+            here = pl.ds(pl.multiple_of((me + ranks - d) % ranks * rows, rows), rows)
+            remote(turned.at[s, d], rhs_ref.at[s, here, :], exchange, (s, d), "freq", (me + d) % ranks).wait_recv()
+        second_step(s, cos_ref, sin_ref, rhs_ref, w_refs[s], me, ranks)
+        for c in range(comps):
+            for way in range(2):
+                hop(s, c, 0, way).start()
+
+    def advance(s, k):
+        for c in range(comps):
+            for way in range(2):
+                landed(s, c, k - 1, way).wait_recv()
+                if k < ranks - 1:
+                    hop(s, c, k, way).start()
+
+    for s in range(segs):
+        for k in range(1, ranks):
+            advance(s, k)
+        pad_edges(w_refs[s], total, ranks)
+
+    for s in range(segs):
+        for d in range(1, ranks):
+            sent(s, d).wait_send()
+        for c in range(comps):
+            for k in range(ranks - 1):
+                for way in range(2):
+                    hop(s, c, k, way).wait_send()
+
+
+def filter_kernel(off_ref, wi_ref, lw_ref, w_first, w_second, band_ref, mine_ref, other_ref, p_ref):
+    half, rows, cols = mine_ref.shape
+    ranks = cols // BLOCK
+    w_refs = (w_first, w_second)
+    scale = 1.0 / (2 * len(w_refs))
+    core = lax.axis_index("seg")
+    weights = [lw_ref[wi_ref[s]] * scale for s in range(len(w_refs))]
+    for out_ref, first in ((other_ref, (1 - core) * half), (mine_ref, core * half)):
+
+        @pl.loop(0, half)
+        def _(i):
+            sums = None
+            for s, w_ref in enumerate(w_refs):
+                got = filter_one(w_ref, band_ref, p_ref.at[s], off_ref, s, first + i, rows, ranks)
+                got = [weights[s] * x for x in got]
+                sums = got if sums is None else [x + y for x, y in zip(sums, got)]
+            for jj in range(ranks):
+                out_ref[i, :, jj * BLOCK : (jj + 1) * BLOCK] = sums[jj].astype(out_ref.dtype)
+
+
+def reversed_taps(kernels):
+    k = kernels.astype(F32)
+    zeros = jnp.zeros(k.shape[:-1] + (k.shape[-1],), F32)
+    return jnp.concatenate([k[..., :1], zeros, jnp.flip(k[..., 1:], -1)], -1)
+
+
+def body(samples, kernels, offsets, weight_index, level_weights):
+    segs, comps, rows, cols = samples.shape
+    ranks = lax.axis_size("freq")
+    size_one = rows * ranks
+    if cols != ranks * BLOCK or rows != BLOCK or size_one != cols or segs != 2 or lax.axis_size("seg") != 2:
+        return general(samples, kernels, offsets, weight_index, level_weights)
+    length = size_one * cols
+    bins = np.arange(cols) - BLOCK // 2
+    near = unit(np.arange(rows)[:, None] * bins[None, :] % length / length, 1.0 / math.sqrt(length))
+    far = unit(np.arange(ranks)[:, None] * rows * bins[None, :] % length / length)
+    half = kernels.shape[1] // 2
+    tall = rows + PAD
+    copies = pltpu.SemaphoreType.DMA
+    gathered = jax.ShapeDtypeStruct((comps, ranks + 1, size_one + tall, BLOCK), BF16)
+    bands = jax.ShapeDtypeStruct((kernels.shape[1], 4 * BLOCK, 2 * BLOCK), BF16)
+    first, second, bands = pl.pallas_call(
+        gather_kernel,
+        out_shape=(gathered, gathered, bands),
+        in_specs=[VMEM] * 14,
+        out_specs=(VMEM, VMEM, VMEM),
+        scratch_shapes=[pltpu.VMEM((cols, cols), BF16)] * 2
+        + [
+            pltpu.VMEM((segs, comps * rows, cols), BF16),
+            pltpu.VMEM((16, cols), F32),
+            pltpu.VMEM((segs, ranks, rows, 2 * BLOCK), BF16),
+            pltpu.VMEM((segs, size_one, 2 * BLOCK), BF16),
+        ]
+        + [copies((segs, ranks))] * 2
+        + [copies((segs, comps, ranks - 1))] * 4,
+        compiler_params=pltpu.CompilerParams(vmem_limit_bytes=36 << 20, collective_id=0, has_side_effects=True),
+    )(
+        samples, reversed_taps(kernels),
+        *wave_bases(cols, -(BLOCK // 2)), *wave_bases(size_one, 0), *near, *far,
+    )
+    mine, other = pl.pallas_call(
+        filter_kernel,
+        out_shape=(
+            jax.ShapeDtypeStruct((half, rows, cols), F32),
+            jax.ShapeDtypeStruct((half, rows, cols), BF16),
+        ),
+        in_specs=[SMEM] * 3 + [VMEM] * 3,
+        out_specs=(VMEM, VMEM),
+        scratch_shapes=[pltpu.VMEM((segs, ranks * tall, BLOCK), F32)],
+        compiler_params=pltpu.CompilerParams(vmem_limit_bytes=28 << 20),
+    )(offsets, weight_index, level_weights, first, second, bands)
+    swapped = lax.ppermute(other, "seg", [(0, 1), (1, 0)])
+    return (mine + swapped.astype(F32)).reshape(half, rows * cols)
+
+
 def solution(mesh):
     in_specs = (
         P(("parts", "seg"), None, "freq", None),

time: 806 us -> 140 us (0.17); the launches traced: 793 us -> 139 us
  waiting for transfers between devices: 283 us -> 2.65 us
  local copies, waits for them, and re-layouts: 251 us -> 14.9 us
  matrix products: 123 us -> 0 us
  Pallas kernels: 0 us -> 121 us
  starting transfers between devices: 92.8 us -> 0.07 us
  other arithmetic: 28.8 us -> 0.4 us
  between operations: 14 us -> 0.07 us
    ppermute x12 -> x1, waiting for transfers between devices: 206 us -> 2.65 us  [body(): swapped = lax.ppermute(other, 'seg', [(0, 1), (1, 0)])]
    dot_general x7 -> x0, matrix products: 123 us -> none  [the longest x1 34.4 us: body(): jnp.dot(stacked, sin_two, precision=highest).reshape(samples.shape)]
    pallas_call x0 -> x2, Pallas kernels: none -> 121 us  [the longest x1 113 us: body(): pl.pallas_call(gather_kernel, out_shape=(gathered, gathered, bands), in_s...]
    another operation x14 -> x0, local copies, waits for them, and re-layouts: 106 us -> none  [the longest x10 100 us: body(): gathered = jnp.stack(received, 0)]
    ppermute x12 -> x1, starting transfers between devices: 81.9 us -> 0.07 us  [body(): swapped = lax.ppermute(other, 'seg', [(0, 1), (1, 0)])]
    gather x81 -> x0, local copies, waits for them, and re-layouts: 71.5 us -> none
    all_to_all x2 -> x0, waiting for transfers between devices: 48.4 us -> none  [the longest x1 24.5 us: body(): lax.all_to_all(second.astype(jnp.bfloat16), 'freq', split_axis=3, concat_...]
    slice x3 -> x2, local copies, waits for them, and re-layouts: 41.4 us -> 1.45 us  [reversed_taps(): return jnp.concatenate([k[..., :1], zeros, jnp.flip(k[..., 1:], -1)], -1)]
  transfers between devices with their start and end apart: 15 -> 1, of which waited for: 7 -> 1; matrix products, arithmetic and copies ran while one was open for 5% -> 0% of each run, Pallas kernels for 0% -> 0%
where the time goes in v2:
time: 140 us; the launch traced here: 139 us
  Pallas kernels  121 us (86%)
  local copies, waits for them, and re-layouts  14.9 us (11%)
  waiting for transfers between devices  2.65 us (2%)
    pallas_call x1, Pallas kernels, body(): pl.pallas_call(gather_kernel, out_shape=(gathered, gathered, bands), in_s...  113 us
    unnamed x29, local copies, waits for them, and re-layouts  13.3 us
    pallas_call x1, Pallas kernels, body(): pl.pallas_call(filter_kernel, out_shape=(jax.ShapeDtypeStruct((half, rows...  8.26 us
  transfers between devices with their start and end apart: 1, of which 1 were waited for; matrix products, arithmetic and copies ran while one was open for 0% of the time, Pallas kernels for 0%

profile of v2, /device:TPU:0, one launch (start us, length us, event | category | flops | bytes accessed | tf_op | source)
XLA Modules:
  0.0 139.3 jit_solution(7848011043672328667)
XLA Ops:
  0.0 0.8 slice.9
  0.8 0.7 slice.8
  1.4 0.1 rev.4
  1.5 0.1 pad.1.clone
  1.6 0.1 pad_maximum_fusion.u_ref
  1.7 0.0 copy-start
  1.7 1.6 %copy-done = f32[2,2,128,1024]{3,2,1,0:T(8,128)S(1)} copy-done((f32[2,2,128,1024]{3,2,1,0:T(8,128)S(1)}, f32[2,2,128,1024]{3,2,1,0:T(8,128)}, u32[]{:S(2)}) %copy-start) | copy-done | bytes 2097176
  3.3 0.0 copy-start.1
  3.3 0.9 copy-done.1
  4.2 0.9 copy-done.2
  5.1 0.0 copy-start.3
  5.1 1.0 copy-done.3
  6.1 0.0 copy-start.4
  6.1 1.0 copy-done.4
  7.2 0.0 copy-start.5
  7.2 0.9 copy-done.5
  8.1 0.0 copy-start.6
  8.1 0.9 copy-done.6
  9.0 0.0 copy-start.7
  9.0 0.9 copy-done.7
  9.9 0.9 copy-done.8
  10.8 0.8 copy-done.9
  11.5 0.8 copy-done.10
  12.3 113.0 %shard_map.163 = (bf16[2,9,1168,128]{3,2,1,0:T(8,128)(2,1)S(1)}, bf16[2,9,1168,128]{3,2,1,0:T(8,128)(2,1)S(1)}, bf16[8,512,256]{2,1,0:T(8,128)(2,1)S(1)}) custom-call(f32[2,2,128,1024]{3,2,1,0:T(8,128)S(1)} %copy-done, f32[2,8,256]{2,1,0:T(8,128)S(1)} %pad_maximum_fusion.u_ref, f32[32,1024]{1,0:T(8,128)S(1)} %copy-done.8, f32[32,1024]{1,0:T(8,128)S(1)} %copy-done.7, ...), custom_call_target="tpu_custom_call" | custom-call | tf_op jit(solution)/shard_map/pallas_call | solution.py:421
  125.3 0.0 copy-done.11
  125.3 0.0 copy-done.12
  125.3 0.0 copy-done.13
  125.3 8.3 %shard_map.164 = (f32[4,128,1024]{2,1,0:T(8,128)S(1)}, bf16[4,128,1024]{2,1,0:T(8,128)(2,1)S(1)}) custom-call(s32[2,8]{1,0:T(2,128)S(1)} %copy-done.11, s32[2]{0:T(128)S(1)} %copy-done.12, f32[16]{0:T(128)S(1)} %copy-done.13, bf16[2,9,1168,128]{3,2,1,0:T(8,128)(2,1)S(1)} %get-tuple-element.10.w_first, ...), custom_call_target="tpu_custom_call" | custom-call | tf_op jit(solution)/shard_map/pallas_call | solution.py:440
  133.6 0.1 collective-permute-start
  133.7 2.6 %collective-permute-done = bf16[4,128,1024]{2,1,0:T(8,128)(2,1)S(1)} collective-permute-done((bf16[4,128,1024]{2,1,0:T(8,128)(2,1)S(1)}, bf16[4,128,1024]{2,1,0:T(8,128)(2,1)S(1)}, u32[]{:S(2)}, u32[]{:S(2)}) %collective-permute-start) | collective-permute-done | bytes 1048608 | tf_op jit(solution)/shard_map/ppermute | solution.py:451
  136.3 0.3 add_bitcast_fusion
  136.7 2.7 %copy.18 = f32[1,4,128,1024]{3,1,2,0:T(4,128)} copy(f32[1,4,128,1024]{3,2,1,0:T(8,128)S(1)} %add_bitcast_fusion) | data formatting | bytes 4194304
  (8 shorter events, 0.0 us)
Async XLA Ops:
  1.7 1.6 %copy-start = (f32[2,2,128,1024]{3,2,1,0:T(8,128)S(1)}, f32[2,2,128,1024]{3,2,1,0:T(8,128)}, u32[]{:S(2)}) copy-start(f32[2,2,128,1024]{3,2,1,0:T(8,128)} %x_ref.1) | copy-start | bytes 6291460
  3.3 0.9 copy-start.1
  4.2 0.9 copy-start.2
  5.1 1.0 copy-start.3
  6.1 1.0 copy-start.4
  7.2 0.9 copy-start.5
  8.1 0.9 copy-start.6
  9.0 0.9 copy-start.7
  9.9 0.9 copy-start.8
  10.8 0.8 copy-start.9
  11.5 0.8 copy-start.10
  12.3 113.0 %copy-start.11 = (s32[2,8]{1,0:T(2,128)S(1)}, s32[2,8]{1,0:T(2,128)}, u32[]{:S(2)}) copy-start(s32[2,8]{1,0:T(2,128)} %off_ref.1) | copy-start | bytes 196
  12.3 113.0 %copy-start.12 = (s32[2]{0:T(128)S(1)}, s32[2]{0:T(128)}, u32[]{:S(2)}) copy-start(s32[2]{0:T(128)} %wi_ref.1) | copy-start | bytes 28
  12.3 113.0 %copy-start.13 = (f32[16]{0:T(128)S(1)}, f32[16]{0:T(128)}, u32[]{:S(2)}) copy-start(f32[16]{0:T(128)} %lw_ref.1) | copy-start | bytes 196
  133.6 2.7 %collective-permute-start = (bf16[4,128,1024]{2,1,0:T(8,128)(2,1)S(1)}, bf16[4,128,1024]{2,1,0:T(8,128)(2,1)S(1)}, u32[]{:S(2)}, u32[]{:S(2)}) collective-permute-start(bf16[4,128,1024]{2,1,0:T(8,128)(2,1)S(1)} %get-tuple-element.14), channel_id=1, source_target_pairs={{0,1},{1,0},{2,3},{3,2},{4,5},{5,4},{6,7},{7,6},{8,9},{9,8},{10,11... | collective-permute-start | bytes 3145736 | tf_op jit(solution)/shard_map/ppermute | solution.py:451

commit v3 on v2

--- a/solution.py
+++ b/solution.py
@@ -188,15 +188,15 @@
         sin_ref[rows, :] = (hs * lc + hc * ls).astype(BF16)
 
 
-def fill_bands(u_ref, band_ref):
+def fill_bands(taps_ref, band_ref):
     wide = 2 * BLOCK
-
-    @pl.loop(0, u_ref.shape[1])
-    def _(t):
+    for t in range(taps_ref.shape[1]):
         both = []
         for c in range(2):
-            row = jnp.broadcast_to(u_ref[c, pl.ds(t, 1), :], (wide, wide))
-            both.append(pltpu.roll(row, 0, 1, stride=1, stride_axis=0)[:, :BLOCK])
+            row = taps_ref[c, t : t + 1, :].astype(F32)
+            row = jnp.concatenate([row, jnp.zeros_like(row)], 1)
+            row = jnp.broadcast_to(row, (BLOCK, wide))
+            both.append(pltpu.roll(row, 0, 1, stride=1, stride_axis=0).T)
         re, im = both
         band_ref[t, :wide, :BLOCK] = re.astype(BF16)
         band_ref[t, :wide, BLOCK:] = im.astype(BF16)
@@ -277,8 +277,8 @@
 
 
 def gather_kernel(
-    x_ref, u_ref,
-    b_lc, b_ls, b_hc, b_hs, e_lc, e_ls, e_hc, e_hs, near_cos, near_sin, far_cos, far_sin,
+    marks,
+    x_ref, table_ref, taps_ref,
     w_first, w_second, band_ref,
     cos_ref, sin_ref, xb_ref, far_ref, turned, rhs_ref,
     ex_send, ex_recv, up_send, up_recv, down_send, down_recv,
@@ -290,6 +290,8 @@
     w_refs = (w_first, w_second)
     exchange = (ex_send, ex_recv)
 
+    tables = [table_ref.at[marks[i] : marks[i + 1], :] for i in range(len(marks) - 1)]
+    b_lc, b_ls, b_hc, b_hs, e_lc, e_ls, e_hc, e_hs, near_cos, near_sin, far_cos, far_sin = tables
     barrier = pltpu.get_barrier_semaphore()
     for d in range(1, ranks):
         peer = (me + d) % ranks
@@ -321,7 +323,7 @@
         rhs_ref[s, own_rows(), :] = step(me)
 
     fill_waves(e_lc, e_ls, e_hc, e_hs, cos_ref, sin_ref)
-    fill_bands(u_ref, band_ref)
+    fill_bands(taps_ref, band_ref)
 
     odd = me % 2
     place = (1 - odd) * (me // 2) + odd * (ranks - 1 - me // 2)
@@ -363,9 +365,10 @@
                 if k < ranks - 1:
                     hop(s, c, k, way).start()
 
+    for k in range(1, ranks):
+        for s in range(segs):
+            advance(s, k)
     for s in range(segs):
-        for k in range(1, ranks):
-            advance(s, k)
         pad_edges(w_refs[s], total, ranks)
 
     for s in range(segs):
@@ -377,30 +380,24 @@
                     hop(s, c, k, way).wait_send()
 
 
-def filter_kernel(off_ref, wi_ref, lw_ref, w_first, w_second, band_ref, mine_ref, other_ref, p_ref):
-    half, rows, cols = mine_ref.shape
+def filter_kernel(own, off_ref, wi_ref, lw_ref, w_first, w_second, band_ref, out_ref, p_ref):
+    half, rows, cols = out_ref.shape
     ranks = cols // BLOCK
     w_refs = (w_first, w_second)
     scale = 1.0 / (2 * len(w_refs))
     core = lax.axis_index("seg")
     weights = [lw_ref[wi_ref[s]] * scale for s in range(len(w_refs))]
-    for out_ref, first in ((other_ref, (1 - core) * half), (mine_ref, core * half)):
-
-        @pl.loop(0, half)
-        def _(i):
-            sums = None
-            for s, w_ref in enumerate(w_refs):
-                got = filter_one(w_ref, band_ref, p_ref.at[s], off_ref, s, first + i, rows, ranks)
-                got = [weights[s] * x for x in got]
-                sums = got if sums is None else [x + y for x, y in zip(sums, got)]
-            for jj in range(ranks):
-                out_ref[i, :, jj * BLOCK : (jj + 1) * BLOCK] = sums[jj].astype(out_ref.dtype)
-
-
-def reversed_taps(kernels):
-    k = kernels.astype(F32)
-    zeros = jnp.zeros(k.shape[:-1] + (k.shape[-1],), F32)
-    return jnp.concatenate([k[..., :1], zeros, jnp.flip(k[..., 1:], -1)], -1)
+    first = (core if own else 1 - core) * half
+
+    @pl.loop(0, half)
+    def _(i):
+        sums = None
+        for s, w_ref in enumerate(w_refs):
+            got = filter_one(w_ref, band_ref, p_ref.at[s], off_ref, s, first + i, rows, ranks)
+            got = [weights[s] * x for x in got]
+            sums = got if sums is None else [x + y for x, y in zip(sums, got)]
+        for jj in range(ranks):
+            out_ref[i, :, jj * BLOCK : (jj + 1) * BLOCK] = sums[jj].astype(out_ref.dtype)
 
 
 def body(samples, kernels, offsets, weight_index, level_weights):
@@ -418,10 +415,12 @@
     copies = pltpu.SemaphoreType.DMA
     gathered = jax.ShapeDtypeStruct((comps, ranks + 1, size_one + tall, BLOCK), BF16)
     bands = jax.ShapeDtypeStruct((kernels.shape[1], 4 * BLOCK, 2 * BLOCK), BF16)
+    tables = (*wave_bases(cols, -(BLOCK // 2)), *wave_bases(size_one, 0), *near, *far)
+    marks = np.cumsum([0] + [len(x) for x in tables]).tolist()
     first, second, bands = pl.pallas_call(
-        gather_kernel,
+        functools.partial(gather_kernel, marks),
         out_shape=(gathered, gathered, bands),
-        in_specs=[VMEM] * 14,
+        in_specs=[VMEM] * 3,
         out_specs=(VMEM, VMEM, VMEM),
         scratch_shapes=[pltpu.VMEM((cols, cols), BF16)] * 2
         + [
@@ -433,23 +432,22 @@
         + [copies((segs, ranks))] * 2
         + [copies((segs, comps, ranks - 1))] * 4,
         compiler_params=pltpu.CompilerParams(vmem_limit_bytes=36 << 20, collective_id=0, has_side_effects=True),
-    )(
-        samples, reversed_taps(kernels),
-        *wave_bases(cols, -(BLOCK // 2)), *wave_bases(size_one, 0), *near, *far,
-    )
-    mine, other = pl.pallas_call(
-        filter_kernel,
-        out_shape=(
-            jax.ShapeDtypeStruct((half, rows, cols), F32),
-            jax.ShapeDtypeStruct((half, rows, cols), BF16),
-        ),
-        in_specs=[SMEM] * 3 + [VMEM] * 3,
-        out_specs=(VMEM, VMEM),
-        scratch_shapes=[pltpu.VMEM((segs, ranks * tall, BLOCK), F32)],
-        compiler_params=pltpu.CompilerParams(vmem_limit_bytes=28 << 20),
-    )(offsets, weight_index, level_weights, first, second, bands)
-    swapped = lax.ppermute(other, "seg", [(0, 1), (1, 0)])
-    return (mine + swapped.astype(F32)).reshape(half, rows * cols)
+    )(samples, np.concatenate(tables), kernels)
+
+    def filtered(own, kind):
+        flops = 2 * 8 * half * segs * ranks * tall * BLOCK * BLOCK
+        return pl.pallas_call(
+            functools.partial(filter_kernel, own),
+            out_shape=jax.ShapeDtypeStruct((half, rows, cols), kind),
+            in_specs=[SMEM] * 3 + [VMEM] * 3,
+            out_specs=VMEM,
+            scratch_shapes=[pltpu.VMEM((segs, ranks * tall, BLOCK), F32)],
+            compiler_params=pltpu.CompilerParams(vmem_limit_bytes=24 << 20),
+            cost_estimate=pl.CostEstimate(flops=flops, bytes_accessed=8 << 20, transcendentals=0),
+        )(offsets, weight_index, level_weights, first, second, bands)
+
+    swapped = lax.ppermute(filtered(False, BF16), "seg", [(0, 1), (1, 0)])
+    return (filtered(True, F32) + swapped.astype(F32)).reshape(half, rows * cols)
 
 
 def solution(mesh):

time: 140 us -> 126 us (0.900)
  local copies, waits for them, and re-layouts: 14.9 us -> 6.57 us
  Pallas kernels: 121 us -> 118 us
  waiting for transfers between devices: 2.65 us -> 0.01 us
    unnamed x29 -> x13, local copies, waits for them, and re-layouts: 13.3 us -> 6.57 us
    pallas_call x2 -> x3, Pallas kernels: 121 us -> 118 us  [the longest x1 109 us: body(): pl.pallas_call(functools.partial(gather_kernel, marks), out_shape=(gather...]
    ppermute x1, waiting for transfers between devices: 2.65 us -> 0.01 us  [body(): swapped = lax.ppermute(filtered(False, BF16), 'seg', [(0, 1), (1, 0)])]
    slice x2 -> x0, local copies, waits for them, and re-layouts: 1.45 us -> none  [reversed_taps(): return jnp.concatenate([k[..., :1], zeros, jnp.flip(k[..., 1:], -1)], -1)]
  transfers between devices with their start and end apart: 1 -> 1, of which waited for: 1 -> 0; matrix products, arithmetic and copies ran while one was open for 0% -> 0% of each run, Pallas kernels for 0% -> 3%
where the time goes in v3:
time: 126 us; the launch traced here: 125 us
  Pallas kernels  118 us (94%)
  local copies, waits for them, and re-layouts  6.57 us (5%)
    pallas_call x1, Pallas kernels, body(): pl.pallas_call(functools.partial(gather_kernel, marks), out_shape=(gather...  109 us
    pallas_call x2, Pallas kernels, filtered(): pl.pallas_call(functools.partial(filter_kernel, own), out_shape=jax.Shape...  8.8 us
    unnamed x13, local copies, waits for them, and re-layouts  6.57 us
  transfers between devices with their start and end apart: 1, of which 0 were waited for; matrix products, arithmetic and copies ran while one was open for 0% of the time, Pallas kernels for 3%

profile of v3, /device:TPU:0, one launch (start us, length us, event | category | flops | bytes accessed | tf_op | source)
XLA Modules:
  0.0 125.3 jit_solution(11831283747423091050)
XLA Ops:
  0.0 0.0 copy-start
  0.0 1.6 %copy-done = f32[528,1024]{1,0:T(8,128)S(1)} copy-done((f32[528,1024]{1,0:T(8,128)S(1)}, f32[528,1024]{1,0:T(8,128)}, u32[]{:S(2)}) %copy-start) | copy-done | bytes 2162712
  1.6 0.0 copy-start.1
  1.6 1.6 %copy-done.1 = f32[2,2,128,1024]{3,2,1,0:T(8,128)S(1)} copy-done((f32[2,2,128,1024]{3,2,1,0:T(8,128)S(1)}, f32[2,2,128,1024]{3,2,1,0:T(8,128)}, u32[]{:S(2)}) %copy-start.1) | copy-done | bytes 2097176
  3.2 0.0 copy-start.2
  3.2 0.7 copy-done.2
  3.9 0.0 copy-start.3
  3.9 0.0 copy-start.4
  3.9 0.0 copy-start.5
  3.9 109.4 %shard_map.64 = (bf16[2,9,1168,128]{3,2,1,0:T(8,128)(2,1)S(1)}, bf16[2,9,1168,128]{3,2,1,0:T(8,128)(2,1)S(1)}, bf16[8,512,256]{2,1,0:T(8,128)(2,1)S(1)}) custom-call(f32[2,2,128,1024]{3,2,1,0:T(8,128)S(1)} %copy-done.1, f32[528,1024]{1,0:T(8,128)S(1)} %copy-done, bf16[2,8,128]{2,1,0:T(8,128)(2,1)S(1)} %copy-done.2), custom_call_target="tpu_custom_call" | custom-call | tf_op jit(solution)/shard_map/pallas_call | solution.py:420
  113.3 0.0 copy-done.3
  113.3 0.0 copy-done.4
  113.3 0.0 copy-done.5
  113.4 4.5 %shard_map.66 = bf16[4,128,1024]{2,1,0:T(8,128)(2,1)S(1)} custom-call(s32[2,8]{1,0:T(2,128)S(1)} %copy-done.3, s32[2]{0:T(128)S(1)} %copy-done.4, f32[16]{0:T(128)S(1)} %copy-done.5, bf16[2,9,1168,128]{3,2,1,0:T(8,128)(2,1)S(1)} %get-tuple-element.8.w_first, bf16[2,9,1168,128]{3,2,1,0:T(8,128)(2,1)S(1)} %get-tuple-element.9.w_second, ...), custom_call_target="tpu_custom_call" | custom-call | flops 2415919104 | bytes 8388608 | tf_op jit(solution)/shard_map/pallas_call | solution.py:439
  117.8 0.1 collective-permute-start
  117.9 4.3 %shard_map.65 = f32[4,128,1024]{2,1,0:T(8,128)S(1)} custom-call(s32[2,8]{1,0:T(2,128)S(1)} %copy-done.3, s32[2]{0:T(128)S(1)} %copy-done.4, f32[16]{0:T(128)S(1)} %copy-done.5, bf16[2,9,1168,128]{3,2,1,0:T(8,128)(2,1)S(1)} %get-tuple-element.8.w_first, bf16[2,9,1168,128]{3,2,1,0:T(8,128)(2,1)S(1)} %get-tuple-element.9.w_second, ...), custom_call_target="tpu_custom_call" | custom-call | flops 2415919104 | bytes 8388608 | tf_op jit(solution)/shard_map/pallas_call | solution.py:439
  122.3 0.0 collective-permute-done
  122.3 0.3 add_bitcast_fusion
  122.6 2.7 %copy.7 = f32[1,4,128,1024]{3,1,2,0:T(4,128)} copy(f32[1,4,128,1024]{3,2,1,0:T(8,128)S(1)} %add_bitcast_fusion) | data formatting | bytes 4194304
Async XLA Ops:
  0.0 1.6 %copy-start = (f32[528,1024]{1,0:T(8,128)S(1)}, f32[528,1024]{1,0:T(8,128)}, u32[]{:S(2)}) copy-start(f32[528,1024]{1,0:T(8,128)} %constant.2.clone.table_ref) | copy-start | bytes 6488068
  1.6 1.6 %copy-start.1 = (f32[2,2,128,1024]{3,2,1,0:T(8,128)S(1)}, f32[2,2,128,1024]{3,2,1,0:T(8,128)}, u32[]{:S(2)}) copy-start(f32[2,2,128,1024]{3,2,1,0:T(8,128)} %x_ref.1) | copy-start | bytes 6291460
  3.2 0.7 copy-start.2
  3.9 109.4 %copy-start.3 = (s32[2,8]{1,0:T(2,128)S(1)}, s32[2,8]{1,0:T(2,128)}, u32[]{:S(2)}) copy-start(s32[2,8]{1,0:T(2,128)} %off_ref.3) | copy-start | bytes 196
  3.9 109.4 %copy-start.4 = (s32[2]{0:T(128)S(1)}, s32[2]{0:T(128)}, u32[]{:S(2)}) copy-start(s32[2]{0:T(128)} %wi_ref.3) | copy-start | bytes 28
  3.9 109.5 %copy-start.5 = (f32[16]{0:T(128)S(1)}, f32[16]{0:T(128)}, u32[]{:S(2)}) copy-start(f32[16]{0:T(128)} %lw_ref.3) | copy-start | bytes 196
  117.8 4.4 %collective-permute-start = (bf16[4,128,1024]{2,1,0:T(8,128)(2,1)S(1)}, bf16[4,128,1024]{2,1,0:T(8,128)(2,1)S(1)}, u32[]{:S(2)}, u32[]{:S(2)}) collective-permute-start(bf16[4,128,1024]{2,1,0:T(8,128)(2,1)S(1)} %shard_map.66), channel_id=1, source_target_pairs={{0,1},{1,0},{2,3},{3,2},{4,5},{5,4},{6,7},{7,6},{8,9},{9,8},{10,11... | collective-permute-start | bytes 3145736 | tf_op jit(solution)/shard_map/ppermute | solution.py:449

commit v4 on v3

--- a/solution.py
+++ b/solution.py
@@ -278,9 +278,10 @@
 
 def gather_kernel(
     marks,
-    x_ref, table_ref, taps_ref,
+    x_hbm, table_hbm, taps_hbm,
     w_first, w_second, band_ref,
-    cos_ref, sin_ref, xb_ref, far_ref, turned, rhs_ref,
+    x_ref, table_ref, taps_ref, cos_ref, sin_ref, xb_ref, far_ref, turned, rhs_ref,
+    in_sem,
     ex_send, ex_recv, up_send, up_recv, down_send, down_recv,
 ):
     segs, comps, rows, cols = x_ref.shape
@@ -290,6 +291,12 @@
     w_refs = (w_first, w_second)
     exchange = (ex_send, ex_recv)
 
+    fetch_table = pltpu.make_async_copy(table_hbm, table_ref, in_sem.at[0])
+    fetch_table.start()
+    fetch_x = pltpu.make_async_copy(x_hbm, x_ref, in_sem.at[1])
+    fetch_x.start()
+    fetch_taps = pltpu.make_async_copy(taps_hbm, taps_ref, in_sem.at[2])
+    fetch_taps.start()
     tables = [table_ref.at[marks[i] : marks[i + 1], :] for i in range(len(marks) - 1)]
     b_lc, b_ls, b_hc, b_hs, e_lc, e_ls, e_hc, e_hs, near_cos, near_sin, far_cos, far_sin = tables
     barrier = pltpu.get_barrier_semaphore()
@@ -298,7 +305,9 @@
         pl.semaphore_signal(barrier, inc=1, device_id={"freq": peer}, device_id_type=pl.DeviceIdType.MESH)
     pl.semaphore_wait(barrier, ranks - 1)
 
+    fetch_table.wait()
     fill_waves(b_lc, b_ls, b_hc, b_hs, cos_ref, sin_ref)
+    fetch_x.wait()
     far_ref[0:1, :] = far_cos[pl.ds(me, 1), :]
     far_ref[8:9, :] = far_sin[pl.ds(me, 1), :]
     for s in range(segs):
@@ -323,6 +332,7 @@
         rhs_ref[s, own_rows(), :] = step(me)
 
     fill_waves(e_lc, e_ls, e_hc, e_hs, cos_ref, sin_ref)
+    fetch_taps.wait()
     fill_bands(taps_ref, band_ref)
 
     odd = me % 2
@@ -348,6 +358,13 @@
         block = w_refs[s].at[c, owner, pl.ds(way * mid, mid), :]
         sems = ((up_send, up_recv), (down_send, down_recv))[way]
         return remote(block, block, sems, (s, c, k), "freq", target)
+
+    def advance(s, k):
+        for c in range(comps):
+            for way in range(2):
+                landed(s, c, k - 1, way).wait_recv()
+                if k < ranks - 1:
+                    hop(s, c, k, way).start()
 
     for s in range(segs):
         for d in range(1, ranks):
@@ -357,19 +374,16 @@
         for c in range(comps):
             for way in range(2):
                 hop(s, c, 0, way).start()
-
-    def advance(s, k):
-        for c in range(comps):
-            for way in range(2):
-                landed(s, c, k - 1, way).wait_recv()
-                if k < ranks - 1:
-                    hop(s, c, k, way).start()
+        if s == 0:
+            advance(0, 1)
 
     for k in range(1, ranks):
-        for s in range(segs):
-            advance(s, k)
-    for s in range(segs):
-        pad_edges(w_refs[s], total, ranks)
+        if k + 1 < ranks:
+            advance(0, k + 1)
+        else:
+            pad_edges(w_refs[0], total, ranks)
+        advance(1, k)
+    pad_edges(w_refs[1], total, ranks)
 
     for s in range(segs):
         for d in range(1, ranks):
@@ -420,19 +434,26 @@
     first, second, bands = pl.pallas_call(
         functools.partial(gather_kernel, marks),
         out_shape=(gathered, gathered, bands),
-        in_specs=[VMEM] * 3,
+        in_specs=[pl.BlockSpec(memory_space=pltpu.HBM)] * 3,
         out_specs=(VMEM, VMEM, VMEM),
-        scratch_shapes=[pltpu.VMEM((cols, cols), BF16)] * 2
+        scratch_shapes=[pltpu.VMEM(samples.shape, F32), pltpu.VMEM((marks[-1], cols), F32)]
+        + [pltpu.VMEM(kernels.shape, kernels.dtype)]
+        + [pltpu.VMEM((cols, cols), BF16)] * 2
         + [
             pltpu.VMEM((segs, comps * rows, cols), BF16),
             pltpu.VMEM((16, cols), F32),
             pltpu.VMEM((segs, ranks, rows, 2 * BLOCK), BF16),
             pltpu.VMEM((segs, size_one, 2 * BLOCK), BF16),
         ]
+        + [copies((3,))]
         + [copies((segs, ranks))] * 2
         + [copies((segs, comps, ranks - 1))] * 4,
         compiler_params=pltpu.CompilerParams(vmem_limit_bytes=36 << 20, collective_id=0, has_side_effects=True),
-    )(samples, np.concatenate(tables), kernels)
+    )(
+        pltpu.with_memory_space_constraint(samples, pltpu.HBM),
+        pltpu.with_memory_space_constraint(jnp.asarray(np.concatenate(tables)), pltpu.HBM),
+        pltpu.with_memory_space_constraint(kernels, pltpu.HBM),
+    )
 
     def filtered(own, kind):
         flops = 2 * 8 * half * segs * ranks * tall * BLOCK * BLOCK

time: 126 us -> 123 us (0.976)
  local copies, waits for them, and re-layouts: 6.57 us -> 2.68 us
  Pallas kernels: 118 us -> 120 us
    unnamed x13 -> x7, local copies, waits for them, and re-layouts: 6.57 us -> 2.68 us
    pallas_call x1, Pallas kernels: 109 us -> 111 us  [body(): pl.pallas_call(functools.partial(gather_kernel, marks), out_shape=(gather...]
  transfers between devices with their start and end apart: 1 -> 1, of which waited for: 0 -> 0; matrix products, arithmetic and copies ran while one was open for 0% -> 0% of each run, Pallas kernels for 3% -> 4%
where the time goes in v4:
time: 123 us
  Pallas kernels  120 us (98%)
  local copies, waits for them, and re-layouts  2.68 us (2%)
    pallas_call x1, Pallas kernels, body(): pl.pallas_call(functools.partial(gather_kernel, marks), out_shape=(gather...  111 us
    pallas_call x2, Pallas kernels, filtered(): pl.pallas_call(functools.partial(filter_kernel, own), out_shape=jax.Shape...  8.79 us
    unnamed x7, local copies, waits for them, and re-layouts  2.68 us
  transfers between devices with their start and end apart: 1, of which 0 were waited for; matrix products, arithmetic and copies ran while one was open for 0% of the time, Pallas kernels for 4%

profile of v4, /device:TPU:0, one launch (start us, length us, event | category | flops | bytes accessed | tf_op | source)
XLA Modules:
  0.0 123.1 jit_solution(15070206587500496537)
XLA Ops:
  0.0 0.0 copy-start.2
  0.0 0.0 copy-start.1
  0.0 0.0 copy-start
  0.0 111.1 %shard_map.64 = (bf16[2,9,1168,128]{3,2,1,0:T(8,128)(2,1)S(1)}, bf16[2,9,1168,128]{3,2,1,0:T(8,128)(2,1)S(1)}, bf16[8,512,256]{2,1,0:T(8,128)(2,1)S(1)}) custom-call(f32[2,2,128,1024]{3,2,1,0:T(8,128)} %x_hbm.1, f32[528,1024]{1,0:T(8,128)} %constant.2.clone.table_hbm, bf16[2,8,128]{2,1,0:T(8,128)(2,1)} %taps_hbm.1), custom_call_target="tpu_custom_call" | custom-call | tf_op jit(solution)/shard_map/pallas_call | solution.py:434
  111.1 0.0 copy-done.2
  111.1 0.0 copy-done.1
  111.1 0.0 copy-done
  111.2 4.5 %shard_map.66 = bf16[4,128,1024]{2,1,0:T(8,128)(2,1)S(1)} custom-call(s32[2,8]{1,0:T(2,128)S(1)} %copy-done, s32[2]{0:T(128)S(1)} %copy-done.1, f32[16]{0:T(128)S(1)} %copy-done.2, bf16[2,9,1168,128]{3,2,1,0:T(8,128)(2,1)S(1)} %get-tuple-element.8.w_first, bf16[2,9,1168,128]{3,2,1,0:T(8,128)(2,1)S(1)} %get-tuple-element.9.w_second, ...), custom_call_target="tpu_custom_call" | custom-call | flops 2415919104 | bytes 8388608 | tf_op jit(solution)/shard_map/pallas_call | solution.py:460
  115.6 0.1 collective-permute-start
  115.7 4.3 %shard_map.65 = f32[4,128,1024]{2,1,0:T(8,128)S(1)} custom-call(s32[2,8]{1,0:T(2,128)S(1)} %copy-done, s32[2]{0:T(128)S(1)} %copy-done.1, f32[16]{0:T(128)S(1)} %copy-done.2, bf16[2,9,1168,128]{3,2,1,0:T(8,128)(2,1)S(1)} %get-tuple-element.8.w_first, bf16[2,9,1168,128]{3,2,1,0:T(8,128)(2,1)S(1)} %get-tuple-element.9.w_second, ...), custom_call_target="tpu_custom_call" | custom-call | flops 2415919104 | bytes 8388608 | tf_op jit(solution)/shard_map/pallas_call | solution.py:460
  120.0 0.0 collective-permute-done
  120.0 0.3 add_bitcast_fusion
  120.4 2.7 %copy.7 = f32[1,4,128,1024]{3,1,2,0:T(4,128)} copy(f32[1,4,128,1024]{3,2,1,0:T(8,128)S(1)} %add_bitcast_fusion) | data formatting | bytes 4194304
Async XLA Ops:
  0.0 111.1 %copy-start.2 = (f32[16]{0:T(128)S(1)}, f32[16]{0:T(128)}, u32[]{:S(2)}) copy-start(f32[16]{0:T(128)} %lw_ref.3) | copy-start | bytes 196
  0.0 111.1 %copy-start.1 = (s32[2]{0:T(128)S(1)}, s32[2]{0:T(128)}, u32[]{:S(2)}) copy-start(s32[2]{0:T(128)} %wi_ref.3) | copy-start | bytes 28
  0.0 111.1 %copy-start = (s32[2,8]{1,0:T(2,128)S(1)}, s32[2,8]{1,0:T(2,128)}, u32[]{:S(2)}) copy-start(s32[2,8]{1,0:T(2,128)} %off_ref.3) | copy-start | bytes 196
  115.6 4.4 %collective-permute-start = (bf16[4,128,1024]{2,1,0:T(8,128)(2,1)S(1)}, bf16[4,128,1024]{2,1,0:T(8,128)(2,1)S(1)}, u32[]{:S(2)}, u32[]{:S(2)}) collective-permute-start(bf16[4,128,1024]{2,1,0:T(8,128)(2,1)S(1)} %shard_map.66), channel_id=1, source_target_pairs={{0,1},{1,0},{2,3},{3,2},{4,5},{5,4},{6,7},{7,6},{8,9},{9,8},{10,11... | collective-permute-start | bytes 3145736 | tf_op jit(solution)/shard_map/ppermute | solution.py:470

commit v5 on v4

--- a/solution.py
+++ b/solution.py
@@ -204,6 +204,19 @@
         band_ref[t, wide:, BLOCK:] = re.astype(BF16)
 
 
+def fill_columns(low_cos, low_sin, high_cos, high_sin, cos_ref, sin_ref, j):
+    step = low_cos.shape[0]
+    lanes = pl.ds(pl.multiple_of(j * BLOCK, BLOCK), BLOCK)
+    lc = low_cos[:, lanes]
+    ls = low_sin[:, lanes]
+    for i in range(high_cos.shape[0]):
+        hc = high_cos[i : i + 1, lanes]
+        hs = high_sin[i : i + 1, lanes]
+        rows = slice(i * step, (i + 1) * step)
+        cos_ref[rows, lanes] = (hc * lc - hs * ls).astype(BF16)
+        sin_ref[rows, lanes] = (hs * lc + hc * ls).astype(BF16)
+
+
 def remote(src, dst, sems, at, axis, device):
     return pltpu.make_async_remote_copy(
         src_ref=src,
@@ -306,7 +319,6 @@
     pl.semaphore_wait(barrier, ranks - 1)
 
     fetch_table.wait()
-    fill_waves(b_lc, b_ls, b_hc, b_hs, cos_ref, sin_ref)
     fetch_x.wait()
     far_ref[0:1, :] = far_cos[pl.ds(me, 1), :]
     far_ref[8:9, :] = far_sin[pl.ds(me, 1), :]
@@ -326,9 +338,13 @@
 
         @pl.loop(1, ranks)
         def _(d):
+            if s == 0:
+                fill_columns(b_lc, b_ls, b_hc, b_hs, cos_ref, sin_ref, (me + d) % ranks)
             turned[s, d] = step((me + d) % ranks)
             sent(s, d).start()
 
+        if s == 0:
+            fill_columns(b_lc, b_ls, b_hc, b_hs, cos_ref, sin_ref, me)
         rhs_ref[s, own_rows(), :] = step(me)
 
     fill_waves(e_lc, e_ls, e_hc, e_hs, cos_ref, sin_ref)

time: 123 us -> 123 us (level)
  no operation moved by 1% of the time
where the time goes in v5:
time: 123 us; the launch traced here: 122 us
  Pallas kernels  119 us (97%)
  local copies, waits for them, and re-layouts  2.68 us (2%)
    pallas_call x1, Pallas kernels, body(): pl.pallas_call(functools.partial(gather_kernel, marks), out_shape=(gather...  110 us
    pallas_call x2, Pallas kernels, filtered(): pl.pallas_call(functools.partial(filter_kernel, own), out_shape=jax.Shape...  8.8 us
    unnamed x7, local copies, waits for them, and re-layouts  2.68 us
  transfers between devices with their start and end apart: 1, of which 0 were waited for; matrix products, arithmetic and copies ran while one was open for 0% of the time, Pallas kernels for 4%

profile of v5, /device:TPU:0, one launch (start us, length us, event | category | flops | bytes accessed | tf_op | source)
XLA Modules:
  0.0 122.4 jit_solution(1673486426568238373)
XLA Ops:
  0.0 0.0 copy-start.2
  0.0 0.0 copy-start.1
  0.0 0.0 copy-start
  0.0 110.4 %shard_map.64 = (bf16[2,9,1168,128]{3,2,1,0:T(8,128)(2,1)S(1)}, bf16[2,9,1168,128]{3,2,1,0:T(8,128)(2,1)S(1)}, bf16[8,512,256]{2,1,0:T(8,128)(2,1)S(1)}) custom-call(f32[2,2,128,1024]{3,2,1,0:T(8,128)} %x_hbm.1, f32[528,1024]{1,0:T(8,128)} %constant.2.clone.table_hbm, bf16[2,8,128]{2,1,0:T(8,128)(2,1)} %taps_hbm.1), custom_call_target="tpu_custom_call" | custom-call | tf_op jit(solution)/shard_map/pallas_call | solution.py:450
  110.4 0.0 copy-done.2
  110.5 0.0 copy-done.1
  110.5 0.0 copy-done
  110.5 4.5 %shard_map.66 = bf16[4,128,1024]{2,1,0:T(8,128)(2,1)S(1)} custom-call(s32[2,8]{1,0:T(2,128)S(1)} %copy-done, s32[2]{0:T(128)S(1)} %copy-done.1, f32[16]{0:T(128)S(1)} %copy-done.2, bf16[2,9,1168,128]{3,2,1,0:T(8,128)(2,1)S(1)} %get-tuple-element.8.w_first, bf16[2,9,1168,128]{3,2,1,0:T(8,128)(2,1)S(1)} %get-tuple-element.9.w_second, ...), custom_call_target="tpu_custom_call" | custom-call | flops 2415919104 | bytes 8388608 | tf_op jit(solution)/shard_map/pallas_call | solution.py:476
  115.0 0.1 collective-permute-start
  115.0 4.3 %shard_map.65 = f32[4,128,1024]{2,1,0:T(8,128)S(1)} custom-call(s32[2,8]{1,0:T(2,128)S(1)} %copy-done, s32[2]{0:T(128)S(1)} %copy-done.1, f32[16]{0:T(128)S(1)} %copy-done.2, bf16[2,9,1168,128]{3,2,1,0:T(8,128)(2,1)S(1)} %get-tuple-element.8.w_first, bf16[2,9,1168,128]{3,2,1,0:T(8,128)(2,1)S(1)} %get-tuple-element.9.w_second, ...), custom_call_target="tpu_custom_call" | custom-call | flops 2415919104 | bytes 8388608 | tf_op jit(solution)/shard_map/pallas_call | solution.py:476
  119.4 0.0 collective-permute-done
  119.4 0.3 add_bitcast_fusion
  119.7 2.7 %copy.7 = f32[1,4,128,1024]{3,1,2,0:T(4,128)} copy(f32[1,4,128,1024]{3,2,1,0:T(8,128)S(1)} %add_bitcast_fusion) | data formatting | bytes 4194304
Async XLA Ops:
  0.0 110.4 %copy-start.2 = (f32[16]{0:T(128)S(1)}, f32[16]{0:T(128)}, u32[]{:S(2)}) copy-start(f32[16]{0:T(128)} %lw_ref.3) | copy-start | bytes 196
  0.0 110.5 %copy-start.1 = (s32[2]{0:T(128)S(1)}, s32[2]{0:T(128)}, u32[]{:S(2)}) copy-start(s32[2]{0:T(128)} %wi_ref.3) | copy-start | bytes 28
  0.0 110.5 %copy-start = (s32[2,8]{1,0:T(2,128)S(1)}, s32[2,8]{1,0:T(2,128)}, u32[]{:S(2)}) copy-start(s32[2,8]{1,0:T(2,128)} %off_ref.3) | copy-start | bytes 196
  115.0 4.4 %collective-permute-start = (bf16[4,128,1024]{2,1,0:T(8,128)(2,1)S(1)}, bf16[4,128,1024]{2,1,0:T(8,128)(2,1)S(1)}, u32[]{:S(2)}, u32[]{:S(2)}) collective-permute-start(bf16[4,128,1024]{2,1,0:T(8,128)(2,1)S(1)} %shard_map.66), channel_id=1, source_target_pairs={{0,1},{1,0},{2,3},{3,2},{4,5},{5,4},{6,7},{7,6},{8,9},{9,8},{10,11... | collective-permute-start | bytes 3145736 | tf_op jit(solution)/shard_map/ppermute | solution.py:486
